TPU v7x, 768 devices: a whole 4x8x12 slice. The times are simulated.
768 devices in a mesh: sub: 96 (over x, z, core), coarse: 8 (over y).
Axes of the slice: x: 4, y: 8, z: 12, core: 2. Of those that a mesh axis runs over, the one named last changes fastest.
Arguments:
- loads: float32 [96, 8, 16, 16, 128], P('sub', 'coarse'), may hold values from -18 to 18
- mode_x: float32 [96, 8, 16, 16], P('sub', 'coarse'), may hold values from -1 to 2
- mode_y: float32 [96, 8, 16, 16], P('sub', 'coarse'), may hold values from -1 to 2
- mode_z: float32 [96, 8, 128, 128], P('sub', 'coarse'), may hold values from -1 to 2
- eigen: float32 [96, 8, 160], P('sub', 'coarse'), may hold values from 0.1 to 2
- classes: int32 [96, 8, 4, 4, 32], P('sub', 'coarse'), may hold values from 0 to 15
- coefficients: float32 [16], replicated, may hold values from 0.25 to 4
- partner: int32 [96, 8, 4, 2], P('sub', 'coarse'), may hold values from 0 to 95, as said below
- rows: int32 [96, 8, 4, 2048], P('sub', 'coarse'), may hold values from 0 to 32767, as said below
- corner_id: int32 [96, 8, 8], P('sub', 'coarse'), may hold values from 0 to 767, as said below
- corner_row: int32 [96, 8, 8], P('sub', 'coarse'), may hold values from 0 to 32767, as said below
- coarse_inverse: float32 [768, 768], P('coarse'), may hold values from -1 to 3, as said below
Outputs:
- multipliers: float32 [96, 8, 4, 2048], P('sub', 'coarse')
- residual: float32 [96, 8, 4, 2048], P('sub', 'coarse')
Inputs may be any that keep to these rules, and one draw needn't show every extreme that they name: partner[i, j, c] differs from (i, j) by one in exactly one index, cyclically; partner[partner[i, j, c], c] = (i, j); the 4 partners of one subdomain are its four cyclic neighbours. `rows`: within one subdomain all 4 x 2048 entries are distinct. `corner_id`: within one subdomain the 8 entries are distinct. `corner_row`: within one subdomain the 8 entries are distinct. `coarse_inverse`: symmetric.
All inputs are finite; a program needn't handle non-finite values.
Results may differ from a plain program's by a relative error of at most 0.0003.
Values sent between devices are 32-bit elements; how exact they have to be, the bound alone decides.
No kernel may reach another device: no remote copies, remote signals or barrier semaphores. Data moves between devices by JAX's collectives and lax.ppermute only.
A program may use at most 32 MiB of HBM per device.

v0:
```python
import jax
import jax.numpy as jnp
from jax import lax
from jax.sharding import PartitionSpec as P

ITERS = 2


def padded_2(x, sides, width):
    for axis, dim in sides:
        size, length = (lax.axis_size(axis), x.shape[dim])
        up = [(i, (i + 1) % size) for i in range(size)]
        down = [(j, i) for i, j in up]
        last = lax.slice_in_dim(x, length - width, length, axis=dim)
        leading = lax.slice_in_dim(x, 0, width, axis=dim)
        before = lax.ppermute(last, axis, up)
        after = lax.ppermute(leading, axis, down)
        x = jnp.concatenate([before, x, after], axis=dim)
    return x


def on_device(
    loads,
    mode_x,
    mode_y,
    mode_z,
    eigen,
    classes,
    coefficients,
    partner,
    rows,
    corner_id,
    corner_row,
    coarse_inverse,
):
    side_x = mode_x[0, 0]
    side_y = mode_y[0, 0]
    side_z = mode_z[0, 0]
    size_x = side_x.shape[0]
    size_y = side_y.shape[0]
    size_z = side_z.shape[0]
    plane = size_x * size_y
    side_pair = (side_x[:, None, :, None] * side_y[None, :, None, :]).reshape(plane, plane)
    spectrum = eigen[0, 0]
    lam_inv = 1.0 / (
        spectrum[:size_x][:, None, None]
        + spectrum[size_x : size_x + size_y][None, :, None]
        + spectrum[size_x + size_y :][None, None, :]
    )
    lam_inv = lam_inv.reshape(plane, size_z)
    class_ids = jnp.arange(coefficients.shape[0], dtype=jnp.int32)
    class_table = class_ids[:, None, None, None] == classes[0, 0][None]
    coef_elem = jnp.sum(jnp.where(class_table, coefficients[:, None, None, None], 0.0), axis=0)
    coef_node = jnp.repeat(jnp.repeat(jnp.repeat(coef_elem, 4, axis=0), 4, axis=1), 4, axis=2)
    inv_root = (1.0 / jnp.sqrt(coef_node)).reshape(plane, size_z)
    sub_count = lax.axis_size("sub")
    column_count = lax.axis_size("coarse")
    myself = lax.axis_index("sub")
    my_column = lax.axis_index("coarse")
    matched = partner[0, 0]
    matched_sub = matched[:, 0]
    matched_col = matched[:, 1]
    sign = jnp.where(
        myself * column_count + my_column < matched_sub * column_count + matched_col, 1.0, -1.0
    ).astype(jnp.float32)[:, None]
    local_rows = rows[0, 0]
    flat_rows = local_rows.reshape(-1)
    corner_nodes = corner_row[0, 0]
    corner_ids = corner_id[0, 0]
    total_corners = coarse_inverse.shape[1]
    nodes = plane * size_z

    def solve(field):
        values = field.reshape(plane, size_z) * inv_root
        values = jnp.einsum("pa,pz->az", side_pair, values, precision=lax.Precision.HIGHEST)
        values = jnp.einsum("xp,pc->xc", values, side_z, precision=lax.Precision.HIGHEST)
        values = values * lam_inv
        values = jnp.einsum("ap,pz->az", side_pair, values, precision=lax.Precision.HIGHEST)
        values = jnp.einsum("xp,cp->xc", values, side_z, precision=lax.Precision.HIGHEST)
        return (values * inv_root).reshape(-1)

    same_column = matched_col == my_column
    same_sub = matched_sub == myself
    prev_sub = same_column & (matched_sub == (myself - 1) % sub_count)
    next_col = same_sub & (matched_col == (my_column + 1) % column_count)
    prev_col = same_sub & (matched_col == (my_column - 1) % column_count)

    def partner_of(values):
        padded = padded_2(values[None, None], (("sub", 0), ("coarse", 1)), 1)
        result = jnp.where(prev_sub[:, None], padded[0, 1], padded[2, 1])
        result = jnp.where(prev_col[:, None], padded[1, 0], result)
        return jnp.where(next_col[:, None], padded[1, 2], result)

    load_field = solve(loads[0, 0].reshape(-1))
    load_values = load_field[local_rows]
    a_rows = coef_node.reshape(-1)[local_rows]
    width = load_values.shape[1]
    far_values = partner_of(jnp.concatenate([load_values, a_rows], axis=1))
    rhs = sign * (load_values - far_values[:, :width])
    a_far = far_values[:, width:]
    weight = a_rows * a_far / (a_rows + a_far)
    multipliers = jnp.zeros_like(rhs)
    residual = rhs

    def precond_dot(resid, pre):
        return lax.psum(jnp.sum(resid * pre), ("sub", "coarse"))

    precond = weight * residual
    direction = precond
    rz_now = precond_dot(residual, precond)
    for step in range(ITERS):
        source = jnp.zeros((nodes,), jnp.float32).at[flat_rows].set((sign * direction).reshape(-1))
        local = solve(source)
        partial_corner = local[corner_nodes]
        corner_table = corner_ids[:, None] == jnp.arange(total_corners, dtype=jnp.int32)[None, :]
        apply_term = jnp.sum(jnp.where(corner_table, partial_corner[:, None], 0.0), axis=0)
        column = lax.psum(apply_term, "sub")
        total = lax.psum(column, "coarse")
        owned = jnp.dot(coarse_inverse, total, precision=lax.Precision.HIGHEST)
        coarse_sol = lax.all_gather(owned, "coarse", axis=0, tiled=True)
        extra = jnp.zeros((nodes,), jnp.float32).at[corner_nodes].set(coarse_sol[corner_ids])
        apply_values = (local + solve(extra))[local_rows]
        image = sign * (apply_values - partner_of(apply_values))
        alpha = rz_now / lax.psum(jnp.sum(direction * image), ("sub", "coarse"))
        multipliers = multipliers + alpha * direction
        residual = residual - alpha * image
        if step + 1 < ITERS:
            precond = weight * residual
            rz_next = precond_dot(residual, precond)
            direction = precond + rz_next / rz_now * direction
            rz_now = rz_next
    return (multipliers[None, None], residual[None, None])


def solution(mesh):
    placed = (
        P("sub", "coarse", None, None, None),
        P("sub", "coarse", None, None),
        P("sub", "coarse", None, None),
        P("sub", "coarse", None, None),
        P("sub", "coarse", None),
        P("sub", "coarse", None, None, None),
        P(),
        P("sub", "coarse", None, None),
        P("sub", "coarse", None, None),
        P("sub", "coarse", None),
        P("sub", "coarse", None),
        P("coarse", None),
    )
    return jax.shard_map(
        on_device,
        mesh=mesh,
        in_specs=placed,
        out_specs=(P("sub", "coarse", None, None), P("sub", "coarse", None, None)),
        check_vma=False,
    )
```

profile of v0, /device:TPU:1, one launch (start us, length us, event | category | flops | bytes accessed | tf_op | source)
XLA Modules:
  0.0 1117.1 jit_solution(7883973808947954249)
XLA Ops:
  3.1 2.6 broadcast_in_dim.155
  5.7 4.9 reshape_reshape.3
  10.6 45.5 %gather_fusion.1 = f32[8192]{0:T(1024)S(1)} fusion(f32[32768]{0:T(1024)S(1)} %reshape_reshape.3, s32[8192]{0:T(1024)S(1)} %broadcast_clamp_fusion), kind=kCustom, calls=%fused_computation.1 | custom fusion | bytes 98304 | tf_op jit(solution)/shard_map/gather | solution.py:96
  58.6 2.5 mul.201
  63.4 45.5 %gather_fusion = f32[8192]{0:T(1024)S(1)} fusion(f32[32768]{0:T(1024)S(1)} %fusion.6, s32[8192]{0:T(1024)S(1)} %broadcast_clamp_fusion), kind=kCustom, calls=%fused_computation | custom fusion | bytes 98304 | tf_op jit(solution)/shard_map/gather | solution.py:95
  108.9 12.4 %collective-permute-start.1 = (f32[1,1,4,4096]{3,2,1,0:T(4,128)S(1)}, f32[1,1,4,4096]{3,2,1,0:T(4,128)S(1)}, u32[]{:S(2)}, u32[]{:S(2)}) collective-permute-start(f32[1,1,4,4096]{3,2,1,0:T(4,128)S(1)} %maximum_bitcast_fusion), channel_id=1, source_target_pairs={{8,0},{16,8},{24,16},{32,24},{40,32},{48,40},{56,48},{64,56},{72,6... | collective-permute-start | bytes 196616 | tf_op jit(solution)/shard_map/ppermute | solution.py:17
  121.4 1.9 collective-permute-start
  125.5 3.8 collective-permute-done
  129.4 3.2 collective-permute-start.3
  132.6 3.8 collective-permute-start.2
  139.2 30.5 %scatter_custom_fusion = f32[32768]{0:T(1024)S(1)} fusion(s32[8192]{0:T(1024)S(1)} %bitcast.215, f32[8192]{0:T(1024)S(1)} %bitcast.218, f32[]{:T(128)} %constant.47.clone.1), kind=kCustom, calls=%fused_computation.76 | custom fusion | bytes 131076 | tf_op jit(solution)/shard_map/scatter | solution.py:112
  172.0 192.5 %psum.57 = f32[768]{0:T(1024)S(1)} all-reduce(f32[768]{0:T(1024)S(1)} %select_reduce_fusion.2), channel_id=1, replica_groups=mesh['sub'=96,'coarse'=8] {'sub'}, use_global_device_ids=true, to_apply=%region_5.6 | all-reduce | flops 768 | bytes 6144 | tf_op jit(solution)/shard_map/psum | solution.py:117
  364.5 14.6 %psum.58 = f32[768]{0:T(1024)S(1)} all-reduce(f32[768]{0:T(1024)S(1)} %psum.57), channel_id=1, replica_groups=mesh['sub'=96,'coarse'=8] {'coarse'}, use_global_device_ids=true, to_apply=%region_6.7 | all-reduce | flops 768 | bytes 6144 | tf_op jit(solution)/shard_map/psum | solution.py:118
  379.5 10.7 all-reduce
  393.3 45.5 %gather_fusion.4 = f32[8192]{0:T(1024)S(1)} fusion(f32[32768]{0:T(1024)S(1)} %fusion.4, s32[8192]{0:T(1024)S(1)} %broadcast_clamp_fusion), kind=kCustom, calls=%fused_computation.4 | custom fusion | bytes 98304 | tf_op jit(solution)/shard_map/gather | solution.py:122
  438.9 5.5 collective-permute-start.4
  444.4 5.9 collective-permute-start.5
  451.1 3.6 collective-permute-start.7
  454.8 3.1 collective-permute-start.6
  458.0 2.2 collective-permute-done.6
  460.9 114.7 %all-reduce.2 = (f32[]{:T(128)}, f32[]{:T(128)}) all-reduce(f32[]{:T(128)} %get-tuple-element.3, f32[]{:T(128)} %get-tuple-element.2), channel_id=1, replica_groups=mesh['sub'=96,'coarse'=8] {'sub','coarse'}, use_global_device_ids=true, to_apply=%region_2.3 | all-reduce | flops 2 | bytes 16 | tf_op jit(solution)/shard_map/psum | solution.py:106
  577.5 103.7 %psum.60 = f32[]{:T(128)} all-reduce(f32[]{:T(128)} %get-tuple-element.8), channel_id=1, replica_groups=mesh['sub'=96,'coarse'=8] {'sub','coarse'}, use_global_device_ids=true, to_apply=%region_11.12 | all-reduce | flops 1 | bytes 8 | tf_op jit(solution)/shard_map/psum | solution.py:106
  682.5 30.5 %scatter_custom_fusion.2 = f32[32768]{0:T(1024)S(1)} fusion(s32[8192]{0:T(1024)S(1)} %bitcast.216, f32[8192]{0:T(1024)S(1)} %bitcast.217, f32[]{:T(128)} %constant.47.clone.1), kind=kCustom, calls=%fused_computation.72 | custom fusion | bytes 131076 | tf_op jit(solution)/shard_map/scatter | solution.py:112
  715.3 185.5 %psum.61 = f32[768]{0:T(1024)S(1)} all-reduce(f32[768]{0:T(1024)S(1)} %select_reduce_fusion.1), channel_id=1, replica_groups=mesh['sub'=96,'coarse'=8] {'sub'}, use_global_device_ids=true, to_apply=%region_14.15 | all-reduce | flops 768 | bytes 6144 | tf_op jit(solution)/shard_map/psum | solution.py:117
  900.8 12.5 %psum.62 = f32[768]{0:T(1024)S(1)} all-reduce(f32[768]{0:T(1024)S(1)} %psum.61), channel_id=1, replica_groups=mesh['sub'=96,'coarse'=8] {'coarse'}, use_global_device_ids=true, to_apply=%region_15.16 | all-reduce | flops 768 | bytes 6144 | tf_op jit(solution)/shard_map/psum | solution.py:118
  913.8 13.0 %all-reduce.1 = f32[768]{0:T(1024)S(1)} all-reduce(f32[768]{0:T(1024)S(1)} %dynamic-update-slice.1), channel_id=1, replica_groups=mesh['sub'=96,'coarse'=8] {'coarse'}, use_global_device_ids=true, to_apply=%add.1 | all-reduce | flops 768 | bytes 6144
  929.7 45.5 %gather_fusion.7 = f32[8192]{0:T(1024)S(1)} fusion(f32[32768]{0:T(1024)S(1)} %fusion.1, s32[8192]{0:T(1024)S(1)} %broadcast_clamp_fusion), kind=kCustom, calls=%fused_computation.7 | custom fusion | bytes 98304 | tf_op jit(solution)/shard_map/gather | solution.py:122
  975.3 9.0 collective-permute-start.8
  984.3 5.9 collective-permute-start.9
  991.0 1.9 collective-permute-start.11
  993.0 4.6 collective-permute-start.10
  999.8 115.3 %psum.63 = f32[]{:T(128)} all-reduce(f32[]{:T(128)} %get-tuple-element.6), channel_id=1, replica_groups=mesh['sub'=96,'coarse'=8] {'sub','coarse'}, use_global_device_ids=true, to_apply=%region_18.19 | all-reduce | flops 1 | bytes 8 | tf_op jit(solution)/shard_map/psum | solution.py:124
  (117 shorter events, 28.8 us)
Async XLA Ops:
  0.6 378.4 %copy-start = (f32[96,768]{1,0:T(8,128)S(1)}, f32[96,768]{1,0:T(8,128)}, u32[]{:S(2)}) copy-start(f32[96,768]{1,0:T(8,128)} %param.23) | copy-start | bytes 884740
  5.7 4.9 copy-start.3
  56.2 0.8 copy-start.4
  56.2 0.8 copy-start.5
  58.6 3.2 copy-start.2
  58.6 3.8 copy-start.1
  63.3 60.1 %copy-start.8 = (s32[1,1,8]{2,1,0:T(1,128)S(1)}, s32[1,1,8]{2,1,0:T(1,128)}, u32[]{:S(2)}) copy-start(s32[1,1,8]{2,1,0:T(1,128)} %param.22) | copy-start | bytes 100
  63.3 60.2 %copy-start.7 = (s32[1,1,8]{2,1,0:T(1,128)S(1)}, s32[1,1,8]{2,1,0:T(1,128)}, u32[]{:S(2)}) copy-start(s32[1,1,8]{2,1,0:T(1,128)} %param.21) | copy-start | bytes 100
  63.3 62.1 %copy-start.6 = (s32[1,1,4,2]{2,3,1,0:T(2,128)S(1)}, s32[1,1,4,2]{2,3,1,0:T(2,128)}, u32[]{:S(2)}) copy-start(s32[1,1,4,2]{2,3,1,0:T(2,128)} %param.19) | copy-start | bytes 100
  108.9 16.6 %collective-permute-start.1 = (f32[1,1,4,4096]{3,2,1,0:T(4,128)S(1)}, f32[1,1,4,4096]{3,2,1,0:T(4,128)S(1)}, u32[]{:S(2)}, u32[]{:S(2)}) collective-permute-start(f32[1,1,4,4096]{3,2,1,0:T(4,128)S(1)} %maximum_bitcast_fusion), channel_id=1, source_target_pairs={{8,0},{16,8},{24,16},{32,24},{40,32},{48,40},{56,48},{64,56},{72,6... | collective-permute-start | bytes 196616 | tf_op jit(solution)/shard_map/ppermute | solution.py:17
  121.4 8.0 collective-permute-start
  129.4 8.1 collective-permute-start.3
  132.6 6.4 collective-permute-start.2
  438.9 11.4 %collective-permute-start.4 = (f32[1,1,4,2048]{3,2,1,0:T(4,128)S(1)}, f32[1,1,4,2048]{3,2,1,0:T(4,128)S(1)}, u32[]{:S(2)}, u32[]{:S(2)}) collective-permute-start(f32[1,1,4,2048]{3,2,1,0:T(4,128)S(1)} %broadcast_in_dim.164), channel_id=1, source_target_pairs={{0,8},{8,16},{16,24},{24,32},{32,40},{40,48},{48,56},{56,64},{64,7... | collective-permute-start | bytes 98312 | tf_op jit(solution)/shard_map/ppermute | solution.py:16
  444.4 6.7 collective-permute-start.5
  451.1 6.8 collective-permute-start.7
  454.8 5.4 collective-permute-start.6
  975.3 14.9 %collective-permute-start.8 = (f32[1,1,4,2048]{3,2,1,0:T(4,128)S(1)}, f32[1,1,4,2048]{3,2,1,0:T(4,128)S(1)}, u32[]{:S(2)}, u32[]{:S(2)}) collective-permute-start(f32[1,1,4,2048]{3,2,1,0:T(4,128)S(1)} %broadcast_in_dim.168), channel_id=1, source_target_pairs={{0,8},{8,16},{16,24},{24,32},{32,40},{40,48},{48,56},{56,64},{64,7... | collective-permute-start | bytes 98312 | tf_op jit(solution)/shard_map/ppermute | solution.py:16
  984.3 6.7 collective-permute-start.9
  991.0 6.6 collective-permute-start.11
  993.0 6.2 collective-permute-start.10
where the time goes:
time: 1120 us
  blocking collectives  763 us (68%)
  local copies, waits for them, and re-layouts  262 us (23%)
  starting transfers between devices  60.9 us (5%)
  waiting for transfers between devices  11.8 us (1%)
    psum x2, blocking collectives, on_device(): column = lax.psum(apply_term, 'sub')  378 us
    psum x2, blocking collectives, precond_dot(): return lax.psum(jnp.sum(resid * pre), ('sub', 'coarse'))  218 us
    psum x1, blocking collectives, on_device(): alpha = rz_now / lax.psum(jnp.sum(direction * image), ('sub', 'coarse'))  115 us
    gather x4, local copies, waits for them, and re-layouts, on_device(): apply_values = (local + solve(extra))[local_rows]  91.1 us
    scatter x2, local copies, waits for them, and re-layouts, on_device(): jnp.zeros((nodes,), jnp.float32).at[flat_rows]  61 us
    gather x2, local copies, waits for them, and re-layouts, on_device(): a_rows = coef_node.reshape(-1)[local_rows]  45.6 us
    gather x2, local copies, waits for them, and re-layouts, on_device(): load_values = load_field[local_rows]  45.6 us
    ppermute x6, starting transfers between devices, padded_2(): after = lax.ppermute(leading, axis, down)  35.7 us
  transfers between devices with their start and end apart: 12, of which 7 were waited for; matrix products, arithmetic and copies ran while one was open for 0% of the time, Pallas kernels for 0%

commit v1 on v0

v1 whole, which is shorter than its diff:
```python
import functools

import jax
import jax.numpy as jnp
import numpy as np
from jax import lax
from jax.experimental import pallas as pl
from jax.experimental.pallas import tpu as pltpu
from jax.sharding import Mesh, PartitionSpec as P

F32 = jnp.float32
BF16 = jnp.bfloat16
I32 = jnp.int32

NX, NZ, NCORE, NY = 4, 12, 2, 8
NSUB = NX * NZ * NCORE
PLANE = 256
DEPTH = 128
COLOURS = 4
WIDTH = 2048
CORNERS = 8
TOTAL = 768
CHUNK = 512
NT = (((1,), (1,)), ((), ()))
TN = (((0,), (0,)), ((), ()))


def iota(shape, dim):
    return lax.broadcasted_iota(I32, shape, dim)


def split(x):
    high = x.astype(BF16)
    return high, (x - high.astype(F32)).astype(BF16)


def dot(a, b, dims=None):
    if dims is None:
        return jnp.dot(a, b, preferred_element_type=F32)
    return lax.dot_general(a, b, dims, preferred_element_type=F32)


def dot_full(a, b, dims=(((1,), (0,)), ((), ()))):
    return lax.dot_general(a, b, dims, precision=lax.Precision.HIGHEST, preferred_element_type=F32)


def product(a, b, dims=None):
    (ah, al), (bh, bl) = a, b
    return dot(ah, bh, dims) + (dot(al, bh, dims) + dot(ah, bl, dims))


def position():
    sub = (lax.axis_index("x") * NZ + lax.axis_index("z")) * NCORE + lax.axis_index("core")
    return sub, lax.axis_index("y")


def colour_of_links(partner_ref):
    sub, col = position()
    odd_sub, odd_col = lax.rem(sub, 2), lax.rem(col, 2)
    mates = (
        (sub + 1 - 2 * odd_sub, col),
        (lax.rem(sub + 2 * odd_sub - 1 + NSUB, NSUB), col),
        (sub, col + 1 - 2 * odd_col),
        (sub, lax.rem(col + 2 * odd_col - 1 + NY, NY)),
    )
    links = []
    for mate_sub, mate_col in mates:
        colour = jnp.int32(0)
        for c in range(1, COLOURS):
            hit = (partner_ref[c, 0] == mate_sub) & (partner_ref[c, 1] == mate_col)
            colour = jnp.where(hit, jnp.int32(c), colour)
        links.append(colour)
    return links


def signs(partner_ref):
    sub, col = position()
    me = sub * NY + col
    which = iota((COLOURS, WIDTH), 0)
    result = jnp.full((COLOURS, WIDTH), 1.0, F32)
    for c in range(COLOURS):
        value = jnp.where(me < partner_ref[c, 0] * NY + partner_ref[c, 1], 1.0, -1.0).astype(F32)
        result = jnp.where(which == c, value, result)
    return result


def by_class(classes, table_ref):
    result = jnp.full(classes.shape, table_ref[0], F32)
    for k in range(1, 16):
        result = jnp.where(classes == k, table_ref[k], result)
    return result


def gather(parts, rows_ref, outs):
    stacked = jnp.concatenate([p for group in parts for p in group], axis=0)
    counts = [len(group) for group in parts]

    def step(j, carry):
        here = pl.ds(pl.multiple_of(j * CHUNK, CHUNK), CHUNK)
        for c in range(COLOURS):
            node = rows_ref[c : c + 1, here]
            hot = (iota((PLANE, CHUNK), 0) == (node >> 7)).astype(F32).astype(BF16)
            mask = iota((DEPTH, CHUNK), 0) == (node & 127)
            picked = dot(stacked, hot)
            at = 0
            for out, count in zip(outs, counts):
                total = picked[at * DEPTH : (at + 1) * DEPTH]
                for extra in range(1, count):
                    total = total + picked[(at + extra) * DEPTH : (at + extra + 1) * DEPTH]
                at += count
                out[c : c + 1, here] = jnp.sum(jnp.where(mask, total, 0.0), axis=0, keepdims=True)
        return carry

    lax.fori_loop(0, WIDTH // CHUNK, step, 0)


def scatter(values_ref, rows_ref):
    def step(j, total):
        here = pl.ds(pl.multiple_of(j * CHUNK, CHUNK), CHUNK)
        for c in range(COLOURS):
            node = rows_ref[c : c + 1, here]
            value = values_ref[c : c + 1, here]
            high = value.astype(BF16).astype(F32)
            hot = (iota((PLANE, CHUNK), 0) == (node >> 7)).astype(F32).astype(BF16)
            mask = iota((DEPTH, CHUNK), 0) == (node & 127)
            left = jnp.concatenate(
                [jnp.where(mask, high, 0.0).astype(BF16), jnp.where(mask, value - high, 0.0).astype(BF16)], axis=0
            )
            total = total + dot(left, hot, NT)
        return total

    total = lax.fori_loop(0, WIDTH // CHUNK, step, jnp.zeros((2 * DEPTH, PLANE), F32))
    return total[:DEPTH] + total[DEPTH:]


def forward(field, planes, depths):
    t = product(split(field), (planes[0], planes[1]))
    return product((depths[2], depths[3]), split(t))


def backward(spectrum, planes, depths):
    t = product(split(spectrum), (planes[2], planes[3]))
    return product((depths[0], depths[1]), split(t))


def kernel_start(
    partner_ref, corner_ref, coef_ref, root_ref,
    loads_ref, mode_x_ref, mode_y_ref, mode_z_ref, eigen_ref, classes_ref, rows_ref,
    planes_ref, depths_ref, fields_ref, corners_ref, near_ref, m0_ref, m1_ref, m2_ref, m3_ref,
    cls_ref,
):
    spread_x = (iota((16, PLANE), 0) == (iota((16, PLANE), 1) >> 4)).astype(F32)
    spread_y = (iota((16, PLANE), 0) == (iota((16, PLANE), 1) & 15)).astype(F32)
    wide_x = dot_full(mode_x_ref[...], spread_x)
    wide_y = dot_full(mode_y_ref[...], spread_y)
    tall_x = dot_full(mode_x_ref[...], spread_x, TN)
    tall_y = dot_full(mode_y_ref[...], spread_y, TN)
    for i in range(16):
        here = slice(16 * i, 16 * i + 16)
        high, low = split(wide_x[i : i + 1] * wide_y)
        planes_ref[0, here], planes_ref[1, here] = high, low
        high, low = split(tall_x[i : i + 1] * tall_y)
        planes_ref[2, here], planes_ref[3, here] = high, low
    mode_z = mode_z_ref[...]
    depths_ref[0], depths_ref[1] = split(mode_z)
    depths_ref[2], depths_ref[3] = split(mode_z.T)
    planes = [planes_ref[i] for i in range(4)]
    depths = [depths_ref[i] for i in range(4)]

    line = dot_full(eigen_ref[:, 0:16], spread_x) + dot_full(eigen_ref[:, 16:32], spread_y)
    diagonal = iota((DEPTH, DEPTH), 0) == iota((DEPTH, DEPTH), 1)
    column = jnp.sum(jnp.where(diagonal, eigen_ref[:, 32:160], 0.0), axis=1, keepdims=True)
    lam_inv = 1.0 / (line + column)
    fields_ref[0] = lam_inv

    spread_c = (iota((16, PLANE), 0) == ((iota((16, PLANE), 1) >> 6) * 4 + ((iota((16, PLANE), 1) >> 2) & 3))).astype(BF16)
    spread_d = (iota((DEPTH, 32), 1) == (iota((DEPTH, 32), 0) >> 2)).astype(BF16)
    small = classes_ref[...].astype(F32).astype(BF16)
    deep = dot(spread_d, small, NT).astype(BF16)
    node_class = dot(deep, spread_c)
    class_part = node_class.astype(BF16)
    root = by_class(node_class.astype(I32), root_ref)
    fields_ref[1] = root

    node = jnp.zeros((CORNERS, 1), I32)
    for t in range(CORNERS):
        node = jnp.where(iota((CORNERS, 1), 0) == t, corner_ref[t], node)
    hot_plane = (iota((CORNERS, PLANE), 1) == (node >> 7)).astype(F32)
    hot_depth = (iota((CORNERS, DEPTH), 1) == (node & 127)).astype(F32)
    hot_p, hot_d = hot_plane.astype(BF16), hot_depth.astype(BF16)
    corner_class = jnp.sum(dot(hot_d, class_part) * hot_plane, axis=1, keepdims=True)
    corner_root = by_class(corner_class.astype(I32), root_ref)
    corners_ref[0:8, :] = dot(hot_p, planes[0]) + dot(hot_p, planes[1])
    corners_ref[8:16, 0:DEPTH] = (dot(hot_d, depths[0]) + dot(hot_d, depths[1])) * corner_root
    corners_ref[8:16, DEPTH:] = jnp.zeros((8, PLANE - DEPTH), F32)

    weights = forward(loads_ref[...].T * root, planes, depths) * lam_inv
    high, low = split(backward(weights, planes, depths) * root)
    gather([(high, low), (class_part,)], rows_ref, [near_ref.at[0], cls_ref])
    near_ref[1] = by_class(cls_ref[...].astype(I32), coef_ref)
    for link, message in zip(colour_of_links(partner_ref), (m0_ref, m1_ref, m2_ref, m3_ref)):
        message[0:1, :] = near_ref[0, pl.ds(link, 1), :]
        message[1:2, :] = near_ref[1, pl.ds(link, 1), :]


def reduce_all(x):
    return jnp.sum(jnp.sum(x, axis=1, keepdims=True), axis=0, keepdims=True)


def launch(ids_ref, rows_ref, x_ref, planes, depths, fields_ref, corners_ref, extras, weights_ref, send_ref):
    lam_inv, root = fields_ref[0], fields_ref[1]
    modes = forward(scatter(x_ref, rows_ref) * root, planes, depths)
    weights = modes * lam_inv
    weights_ref[...] = weights
    energy = reduce_all(weights * modes)
    part = dot_full(corners_ref[0:8, :], weights, NT) * corners_ref[8:16, 0:DEPTH]
    part = jnp.sum(part, axis=1, keepdims=True)
    place = iota((8, 128), 0) * 128 + iota((8, 128), 1)
    tile = jnp.zeros((8, 128), F32)
    for t in range(CORNERS):
        tile = tile + jnp.where(place == ids_ref[t], part[t : t + 1, 0:1], 0.0)
    for at, scalar in enumerate([energy] + extras):
        tile = jnp.where(place == TOTAL + at, scalar, tile)
    send_ref[...] = jnp.broadcast_to(tile[None], send_ref.shape)


def receive(partner_ref, messages, far_ref):
    count = messages[0].shape[0]
    for link, message in zip(colour_of_links(partner_ref), messages):
        for i in range(count):
            far_ref[i, pl.ds(link, 1), :] = message[i : i + 1, :]


def kernel_first(
    partner_ref, ids_ref, rows_ref, near_ref, m0_ref, m1_ref, m2_ref, m3_ref,
    planes_ref, depths_ref, fields_ref, corners_ref,
    state_ref, weights_ref, send_ref,
    far_ref, x_ref,
):
    receive(partner_ref, (m0_ref, m1_ref, m2_ref, m3_ref), far_ref)
    sign = signs(partner_ref)
    a, a_far = near_ref[1], far_ref[1]
    rhs = sign * (near_ref[0] - far_ref[0])
    weight = a * a_far / (a + a_far)
    precond = weight * rhs
    state_ref[0] = rhs
    state_ref[1] = weight
    x_ref[...] = sign * precond
    planes = [planes_ref[i] for i in range(4)]
    depths = [depths_ref[i] for i in range(4)]
    launch(
        ids_ref, rows_ref, x_ref, planes, depths, fields_ref, corners_ref, [reduce_all(rhs * precond)],
        weights_ref, send_ref,
    )


def kernel_relay(got_ref, send_ref):
    tile = jnp.sum(got_ref[...], axis=0)
    send_ref[...] = jnp.broadcast_to(tile[None], send_ref.shape)


def kernel_coarse(
    partner_ref, ids_ref, rows_ref, got_ref, inverse_ref, weights_ref,
    planes_ref, depths_ref, fields_ref, corners_ref,
    near_ref, sums_ref, m0_ref, m1_ref, m2_ref, m3_ref,
):
    tile = jnp.sum(got_ref[...], axis=0)
    line = jnp.concatenate([tile[i : i + 1] for i in range(TOTAL // 128)], axis=1)
    high = line.astype(BF16).astype(F32)
    middle = (line - high).astype(BF16).astype(F32)
    low = line - high - middle
    which = iota((8, TOTAL), 0)
    left = jnp.where(which == 0, high, jnp.where(which == 1, middle, jnp.where(which == 2, low, 0.0))).astype(BF16)
    inverse_high, inverse_low = split(inverse_ref[...])
    coarse = jnp.sum(dot(left, inverse_high) + dot(left, inverse_low), axis=0, keepdims=True)
    work = reduce_all(coarse * line)
    scalars = tile[6:7, :]
    sums = jnp.where(iota((8, 128), 1) == 3, work, jnp.broadcast_to(scalars, (8, 128)))
    sums_ref[...] = sums
    ids = jnp.zeros((CORNERS, 1), I32)
    for t in range(CORNERS):
        ids = jnp.where(iota((CORNERS, 1), 0) == t, ids_ref[t], ids)
    own = jnp.sum(jnp.where(iota((CORNERS, TOTAL), 1) == ids, coarse, 0.0), axis=1, keepdims=True)
    lam_inv, root = fields_ref[0], fields_ref[1]
    lifted = dot_full(corners_ref[8:16, 0:DEPTH] * own, corners_ref[0:8, :], TN)
    weights = weights_ref[...] + lam_inv * lifted
    planes = [planes_ref[i] for i in range(4)]
    depths = [depths_ref[i] for i in range(4)]
    high, low = split(backward(weights, planes, depths) * root)
    gather([(high, low)], rows_ref, [near_ref])
    for link, message in zip(colour_of_links(partner_ref), (m0_ref, m1_ref, m2_ref, m3_ref)):
        message[...] = near_ref[pl.ds(link, 1), :]


def kernel_second(
    partner_ref, ids_ref, rows_ref, near_ref, sums_ref, m0_ref, m1_ref, m2_ref, m3_ref, state_ref,
    planes_ref, depths_ref, fields_ref, corners_ref,
    later_ref, weights_ref, send_ref,
    far_ref, x_ref,
):
    receive(partner_ref, (m0_ref, m1_ref, m2_ref, m3_ref), far_ref)
    sign = signs(partner_ref)
    image = sign * (near_ref[...] - far_ref[0])
    energy, rz, work = sums_ref[0:1, 0:1], sums_ref[0:1, 1:2], sums_ref[0:1, 3:4]
    alpha = rz / (2.0 * (energy + work))
    rhs, weight = state_ref[0], state_ref[1]
    residual = rhs - alpha * image
    precond = weight * residual
    later_ref[0] = image
    later_ref[1] = residual
    later_ref[2] = precond
    later_ref[3] = weight * rhs
    x_ref[...] = sign * precond
    planes = [planes_ref[i] for i in range(4)]
    depths = [depths_ref[i] for i in range(4)]
    launch(
        ids_ref, rows_ref, x_ref, planes, depths, fields_ref, corners_ref,
        [reduce_all(residual * precond), reduce_all(precond * image)], weights_ref, send_ref,
    )


def kernel_end(
    partner_ref, near_ref, sums_ref, first_ref, m0_ref, m1_ref, m2_ref, m3_ref, later_ref,
    multipliers_ref, residual_ref,
    far_ref,
):
    receive(partner_ref, (m0_ref, m1_ref, m2_ref, m3_ref), far_ref)
    sign = signs(partner_ref)
    energy, rz, work = first_ref[0:1, 0:1], first_ref[0:1, 1:2], first_ref[0:1, 3:4]
    form = 2.0 * (energy + work)
    alpha = rz / form
    energy, rz_next, cross, work = (sums_ref[0:1, i : i + 1] for i in range(4))
    beta = rz_next / rz
    form_next = 2.0 * (energy + work) + beta * (2.0 * cross + beta * form)
    alpha_next = rz_next / form_next
    image, residual, precond, direction = (later_ref[i] for i in range(4))
    image_next = sign * (near_ref[...] - far_ref[0]) + beta * image
    direction_next = precond + beta * direction
    multipliers_ref[...] = alpha * direction + alpha_next * direction_next
    residual_ref[...] = residual - alpha_next * image_next


VMEM = pl.BlockSpec(memory_space=pltpu.VMEM)
SMEM = pl.BlockSpec(memory_space=pltpu.SMEM)


def call(kernel, name, scalars, arrays, outs, scratch=(), flops=2_000_000_000):
    shapes = [jax.ShapeDtypeStruct(*o) for o in outs]
    return pl.pallas_call(
        kernel,
        name=name,
        out_shape=shapes,
        in_specs=[SMEM] * len(scalars) + [VMEM] * len(arrays),
        out_specs=[VMEM] * len(outs),
        scratch_shapes=[pltpu.VMEM(*s) for s in scratch],
        compiler_params=pltpu.CompilerParams(vmem_limit_bytes=40 * 1024 * 1024),
        cost_estimate=pl.CostEstimate(flops=flops, bytes_accessed=4_000_000, transcendentals=0),
    )(*scalars, *arrays)


def pairing(size, first):
    pairs = []
    for i in range(first, size + first, 2):
        a, b = i % size, (i + 1) % size
        pairs += [(a, b), (b, a)]
    return pairs


def exchange(messages):
    sub = ("x", "z", "core")
    near_sub = lax.ppermute(messages[0], sub, pairing(NSUB, 0))
    far_sub = lax.ppermute(messages[1], sub, pairing(NSUB, 1))
    near_col = lax.ppermute(messages[2], "y", pairing(NY, 0))
    far_col = lax.ppermute(messages[3], "y", pairing(NY, 1))
    return near_sub, far_sub, near_col, far_col


def spread(send, axes, count):
    return lax.all_to_all(send.reshape(count * 8, 128), axes, 0, 0, tiled=True).reshape(count, 8, 128)


def on_device(
    loads, mode_x, mode_y, mode_z, eigen, classes, coefficients, partner, rows, corner_id, corner_row, coarse_inverse
):
    inverse = lax.all_gather(coarse_inverse, "y", axis=0, tiled=True)
    rows = rows[0, 0]
    partner = partner[0, 0]
    ids = corner_id[0, 0]
    halo = (2, WIDTH)
    one = (1, WIDTH)
    wide = (COLOURS, WIDTH)
    planes, depths, fields, corners, near, *messages = call(
        kernel_start,
        "start",
        [partner, corner_row[0, 0], coefficients, 1.0 / jnp.sqrt(coefficients)],
        [
            loads.reshape(PLANE, DEPTH), mode_x[0, 0], mode_y[0, 0], mode_z[0, 0], eigen[0],
            classes.reshape(16, 32), rows,
        ],
        [
            ((4, PLANE, PLANE), BF16), ((4, DEPTH, DEPTH), BF16), ((2, DEPTH, PLANE), F32), ((16, PLANE), F32),
            ((2, *wide), F32), (halo, F32), (halo, F32), (halo, F32), (halo, F32),
        ],
        [(wide, F32)],
    )
    shared = [planes, depths, fields, corners]
    messages = exchange(messages)

    def total(send):
        got = spread(send, ("z", "core"), NZ * NCORE)
        (send,) = call(kernel_relay, "relay", [], [got], [((NX * NY, 8, 128), F32)], flops=1000)
        return spread(send, ("x", "y"), NX * NY)

    weights_out = ((DEPTH, PLANE), F32)
    send_out = ((NZ * NCORE, 8, 128), F32)
    scratch = [((2, *wide), F32), (wide, F32)]
    state, weights, send = call(
        kernel_first, "first", [partner, ids], [rows, near, *messages, *shared],
        [((2, *wide), F32), weights_out, send_out], scratch,
    )
    coarse_outs = [(wide, F32), ((8, 128), F32), (one, F32), (one, F32), (one, F32), (one, F32)]
    got = total(send)
    near, first_sums, *messages = call(
        kernel_coarse, "coarse", [partner, ids], [rows, got, inverse, weights, *shared], coarse_outs
    )
    messages = exchange(messages)
    later, weights, send = call(
        kernel_second, "second", [partner, ids], [rows, near, first_sums, *messages, state, *shared],
        [((4, *wide), F32), weights_out, send_out], scratch,
    )
    got = total(send)
    near, sums, *messages = call(
        kernel_coarse, "coarse", [partner, ids], [rows, got, inverse, weights, *shared], coarse_outs
    )
    messages = exchange(messages)
    multipliers, residual = call(
        kernel_end, "end", [partner], [near, sums, first_sums, *messages, later], [(wide, F32), (wide, F32)],
        scratch[:1], flops=1000,
    )
    return multipliers[None, None], residual[None, None]


def solution(mesh):
    fine = Mesh(np.asarray(mesh.devices).reshape(NX, NZ, NCORE, NY), ("x", "z", "core", "y"))
    sub = ("x", "z", "core")
    placed = (
        P(sub, "y", None, None, None),
        P(sub, "y", None, None),
        P(sub, "y", None, None),
        P(sub, "y", None, None),
        P(sub, "y", None),
        P(sub, "y", None, None, None),
        P(),
        P(sub, "y", None, None),
        P(sub, "y", None, None),
        P(sub, "y", None),
        P(sub, "y", None),
        P("y", None),
    )
    return jax.shard_map(
        on_device,
        mesh=fine,
        in_specs=placed,
        out_specs=(P(sub, "y", None, None), P(sub, "y", None, None)),
        check_vma=False,
    )
```

time: 1120 us -> 169 us (0.15)
  blocking collectives: 763 us -> 68 us
  local copies, waits for them, and re-layouts: 262 us -> 9.68 us
  Pallas kernels: 0 us -> 22.6 us
  starting transfers between devices: 60.9 us -> 40.7 us
    psum x7 -> x0, blocking collectives: 739 us -> none  [the longest x2 378 us: on_device(): column = lax.psum(apply_term, 'sub')]
    gather x12 -> x0, local copies, waits for them, and re-layouts: 185 us -> none  [the longest x4 91.1 us: on_device(): apply_values = (local + solve(extra))[local_rows]]
    all_to_all x0 -> x4, blocking collectives: none -> 68 us  [spread(): lax.all_to_all(send.reshape(count * 8, 128), axes, 0, 0, tiled=True)]
    scatter x4 -> x0, local copies, waits for them, and re-layouts: 62.5 us -> none  [the longest x2 61 us: on_device(): jnp.zeros((nodes,), jnp.float32).at[flat_rows]]
    unnamed x2 -> x0, blocking collectives: 23.8 us -> none
    pallas_call x0 -> x8, Pallas kernels: none -> 22.6 us  [call(): pl.pallas_call(kernel, name=name, out_shape=shapes, in_specs=[SMEM] * len...]
    ppermute x12, starting transfers between devices: 60.9 us -> 40.6 us  [the longest x3 20.5 us: exchange(): near_sub = lax.ppermute(messages[0], sub, pairing(NSUB, 0))]
  transfers between devices with their start and end apart: 12 -> 13, of which waited for: 7 -> 4; matrix products, arithmetic and copies ran while one was open for 0% -> 1% of each run, Pallas kernels for 0% -> 5%
where the time goes in v1:
time: 169 us; the launch traced here: 167 us
  blocking collectives  68 us (40%)
  starting transfers between devices  40.7 us (24%)
  Pallas kernels  22.6 us (13%)
  between operations  14.2 us (8%)
  waiting for transfers between devices  11.6 us (7%)
  local copies, waits for them, and re-layouts  9.68 us (6%)
    all_to_all x4, blocking collectives, spread(): lax.all_to_all(send.reshape(count * 8, 128), axes, 0, 0, tiled=True)  68 us
    pallas_call x8, Pallas kernels, call(): pl.pallas_call(kernel, name=name, out_shape=shapes, in_specs=[SMEM] * len...  22.6 us
    ppermute x3, starting transfers between devices, exchange(): near_sub = lax.ppermute(messages[0], sub, pairing(NSUB, 0))  20.5 us
    ppermute x3, waiting for transfers between devices, exchange(): far_col = lax.ppermute(messages[3], 'y', pairing(NY, 1))  9.52 us
    unnamed x26, local copies, waits for them, and re-layouts  8.25 us
    ppermute x3, starting transfers between devices, exchange(): near_col = lax.ppermute(messages[2], 'y', pairing(NY, 0))  7.68 us
    ppermute x3, starting transfers between devices, exchange(): far_col = lax.ppermute(messages[3], 'y', pairing(NY, 1))  6.38 us
    ppermute x3, starting transfers between devices, exchange(): far_sub = lax.ppermute(messages[1], sub, pairing(NSUB, 1))  6.11 us
  transfers between devices with their start and end apart: 13, of which 4 were waited for; matrix products, arithmetic and copies ran while one was open for 1% of the time, Pallas kernels for 5%

profile of v1, /device:TPU:1, one launch (start us, length us, event | category | flops | bytes accessed | tf_op | source)
XLA Modules:
  0.0 166.7 jit_solution(16753482930770926422)
XLA Ops:
  8.6 0.8 copy.19.partner_ref
  9.3 0.9 copy-done.2
  10.2 0.8 copy-done.3
  11.1 0.8 copy-done.4
  11.8 0.7 copy-done.6
  15.9 4.6 %start.1 = (bf16[4,256,256]{2,1,0:T(8,128)(2,1)S(1)}, bf16[4,128,128]{2,1,0:T(8,128)(2,1)S(1)}, f32[2,128,256]{2,1,0:T(8,128)S(1)}, f32[16,256]{1,0:T(8,128)S(1)...) custom-call(s32[4,2]{1,0:T(4,128)S(1)} %copy.19.partner_ref, ...), custom_call_target="tpu_custom_call" | custom-call | flops 2000000000 | bytes 4000000 | tf_op jit(solution)/shard_map/start/pallas_call | solution.py:349
  20.5 12.4 %collective-permute-start = (f32[2,2048]{1,0:T(2,128)S(1)}, f32[2,2048]{1,0:T(2,128)S(1)}, u32[]{:S(2)}, u32[]{:S(2)}) collective-permute-start(f32[2,2048]{1,0:T(2,128)S(1)} %get-tuple-element.32), channel_id=1, source_target_pairs={{0,8},{8,0},{16,24},{24,16},{32,40},{40,32},{48,56},{56,48},{64,72... | collective-permute-start | bytes 49160 | tf_op jit(solution)/shard_map/ppermute | solution.py:371
  32.9 1.9 %collective-permute-start.1 = (f32[2,2048]{1,0:T(2,128)S(1)}, f32[2,2048]{1,0:T(2,128)S(1)}, u32[]{:S(2)}, u32[]{:S(2)}) collective-permute-start(f32[2,2048]{1,0:T(2,128)S(1)} %get-tuple-element.33), channel_id=1, source_target_pairs={{8,16},{16,8},{24,32},{32,24},{40,48},{48,40},{56,64},{64,56},{72,... | collective-permute-start | bytes 49160 | tf_op jit(solution)/shard_map/ppermute | solution.py:372
  34.9 1.9 %collective-permute-start.2 = (f32[2,2048]{1,0:T(2,128)S(1)}, f32[2,2048]{1,0:T(2,128)S(1)}, u32[]{:S(2)}, u32[]{:S(2)}) collective-permute-start(f32[2,2048]{1,0:T(2,128)S(1)} %get-tuple-element.34), channel_id=1, source_target_pairs={{0,1},{1,0},{2,3},{3,2},{4,5},{5,4},{6,7},{7,6},{8,9},{9,8},{10,11... | collective-permute-start | bytes 49160 | tf_op jit(solution)/shard_map/ppermute | solution.py:373
  36.8 1.9 %collective-permute-start.3 = (f32[2,2048]{1,0:T(2,128)S(1)}, f32[2,2048]{1,0:T(2,128)S(1)}, u32[]{:S(2)}, u32[]{:S(2)}) collective-permute-start(f32[2,2048]{1,0:T(2,128)S(1)} %get-tuple-element.35), channel_id=1, source_target_pairs={{1,2},{2,1},{3,4},{4,3},{5,6},{6,5},{7,0},{0,7},{9,10},{10,9},{11,... | collective-permute-start | bytes 49160 | tf_op jit(solution)/shard_map/ppermute | solution.py:374
  38.7 1.3 collective-permute-done.2.m2_ref
  40.1 2.9 %collective-permute-done.3.m3_ref = f32[2,2048]{1,0:T(2,128)S(1)} collective-permute-done((f32[2,2048]{1,0:T(2,128)S(1)}, f32[2,2048]{1,0:T(2,128)S(1)}, u32[]{:S(2)}, u32[]{:S(2)}) %collective-permute-start.3) | collective-permute-done | bytes 16416 | tf_op jit(solution)/shard_map/ppermute | solution.py:374
  42.9 3.8 %first.1 = (f32[2,4,2048]{2,1,0:T(4,128)S(1)}, f32[128,256]{1,0:T(8,128)S(1)}, f32[24,8,128]{2,1,0:T(8,128)S(1)}) custom-call(s32[4,2]{1,0:T(4,128)S(1)} %copy.19.partner_ref, s32[8]{0:T(128)S(1)} %bitcast.24, s32[4,2048]{1,0:T(4,128)S(1)} %bitcast.15, f32[2,4,2048]{2,1,0:T(4,128)S(1)} %get-tuple-element.31.near_ref, ...), custom_call_target="tpu_custom_call" | custom-call | flops 2000000000 | bytes 4000000 | tf_op jit(solution)/shard_map/first/pallas_call | solution.py:349
  46.8 22.0 %all_to_all.24.got_ref = f32[24,8,128]{2,1,0:T(8,128)S(1)} all-to-all(f32[24,8,128]{2,1,0:T(8,128)S(1)} %get-tuple-element.40), channel_id=1, replica_groups=mesh['x'=4,'z'=12,'core'=2,'y'=8] {'z','core'}, dimensions={0} | all-to-all | bytes 196608 | tf_op jit(solution)/shard_map/all_to_all | solution.py:379
  68.9 15.7 %all_to_all.25.got_ref = f32[32,8,128]{2,1,0:T(8,128)S(1)} all-to-all(f32[32,8,128]{2,1,0:T(8,128)S(1)} %relay.2), channel_id=1, replica_groups=mesh['x'=4,'z'=12,'core'=2,'y'=8] {'x','y'}, dimensions={0} | all-to-all | bytes 262144 | tf_op jit(solution)/shard_map/all_to_all | solution.py:379
  84.5 1.7 copy-done
  86.2 4.2 %coarse.2 = (f32[4,2048]{1,0:T(4,128)S(1)}, f32[8,128]{1,0:T(8,128)S(1)}, f32[1,2048]{1,0:T(1,128)S(1)}, f32[1,2048]{1,0:T(1,128)S(1)}, f32[1,2048]{1,0:T(1,128)S(1)}, /*index=5*/f32[1,2048]{1,0:T(1,128)S(1)}) custom-call(s32[4,2]{1,0:T(4,128)S(1)} %copy.19.partner_ref, s32[8]{0:T(128)S(1)} %bitcast.25, s32[4,2048]{1,0:T(4,128)S(1)} %bitcast.16, ...), custom_call_target="tpu_custom_call" | custom-call | flops 2000000000 | bytes 4000000 | tf_op jit(solution)/shard_map/coarse/pallas_call | solution.py:349
  90.4 4.1 %collective-permute-start.4 = (f32[1,2048]{1,0:T(1,128)S(1)}, f32[1,2048]{1,0:T(1,128)S(1)}, u32[]{:S(2)}, u32[]{:S(2)}) collective-permute-start(f32[1,2048]{1,0:T(1,128)S(1)} %get-tuple-element.44), channel_id=1, source_target_pairs={{0,8},{8,0},{16,24},{24,16},{32,40},{40,32},{48,56},{56,48},{64,72... | collective-permute-start | bytes 24584 | tf_op jit(solution)/shard_map/ppermute | solution.py:371
  94.4 2.1 %collective-permute-start.5 = (f32[1,2048]{1,0:T(1,128)S(1)}, f32[1,2048]{1,0:T(1,128)S(1)}, u32[]{:S(2)}, u32[]{:S(2)}) collective-permute-start(f32[1,2048]{1,0:T(1,128)S(1)} %get-tuple-element.45), channel_id=1, source_target_pairs={{8,16},{16,8},{24,32},{32,24},{40,48},{48,40},{56,64},{64,56},{72,... | collective-permute-start | bytes 24584 | tf_op jit(solution)/shard_map/ppermute | solution.py:372
  96.6 2.9 %collective-permute-start.6 = (f32[1,2048]{1,0:T(1,128)S(1)}, f32[1,2048]{1,0:T(1,128)S(1)}, u32[]{:S(2)}, u32[]{:S(2)}) collective-permute-start(f32[1,2048]{1,0:T(1,128)S(1)} %get-tuple-element.46), channel_id=1, source_target_pairs={{0,1},{1,0},{2,3},{3,2},{4,5},{5,4},{6,7},{7,6},{8,9},{9,8},{10,11... | collective-permute-start | bytes 24584 | tf_op jit(solution)/shard_map/ppermute | solution.py:373
  99.5 2.2 %collective-permute-start.7 = (f32[1,2048]{1,0:T(1,128)S(1)}, f32[1,2048]{1,0:T(1,128)S(1)}, u32[]{:S(2)}, u32[]{:S(2)}) collective-permute-start(f32[1,2048]{1,0:T(1,128)S(1)} %get-tuple-element.47), channel_id=1, source_target_pairs={{1,2},{2,1},{3,4},{4,3},{5,6},{6,5},{7,0},{0,7},{9,10},{10,9},{11,... | collective-permute-start | bytes 24584 | tf_op jit(solution)/shard_map/ppermute | solution.py:374
  101.7 3.3 %collective-permute-done.7.m3_ref = f32[1,2048]{1,0:T(1,128)S(1)} collective-permute-done((f32[1,2048]{1,0:T(1,128)S(1)}, f32[1,2048]{1,0:T(1,128)S(1)}, u32[]{:S(2)}, u32[]{:S(2)}) %collective-permute-start.7) | collective-permute-done | bytes 8224 | tf_op jit(solution)/shard_map/ppermute | solution.py:374
  105.1 4.0 %second.1 = (f32[4,4,2048]{2,1,0:T(4,128)S(1)}, f32[128,256]{1,0:T(8,128)S(1)}, f32[24,8,128]{2,1,0:T(8,128)S(1)}) custom-call(s32[4,2]{1,0:T(4,128)S(1)} %copy.19.partner_ref, s32[8]{0:T(128)S(1)} %bitcast.26, s32[4,2048]{1,0:T(4,128)S(1)} %bitcast.17, f32[4,2048]{1,0:T(4,128)S(1)} %get-tuple-element.42.near_ref, ...), custom_call_target="tpu_custom_call" | custom-call | flops 2000000000 | bytes 4000000 | tf_op jit(solution)/shard_map/second/pallas_call | solution.py:349
  109.1 17.6 %all_to_all.26.got_ref = f32[24,8,128]{2,1,0:T(8,128)S(1)} all-to-all(f32[24,8,128]{2,1,0:T(8,128)S(1)} %get-tuple-element.49), channel_id=1, replica_groups=mesh['x'=4,'z'=12,'core'=2,'y'=8] {'z','core'}, dimensions={0} | all-to-all | bytes 196608 | tf_op jit(solution)/shard_map/all_to_all | solution.py:379
  126.8 12.6 %all_to_all.27.got_ref = f32[32,8,128]{2,1,0:T(8,128)S(1)} all-to-all(f32[32,8,128]{2,1,0:T(8,128)S(1)} %relay.3), channel_id=1, replica_groups=mesh['x'=4,'z'=12,'core'=2,'y'=8] {'x','y'}, dimensions={0} | all-to-all | bytes 262144 | tf_op jit(solution)/shard_map/all_to_all | solution.py:379
  139.4 4.2 %coarse.3 = (f32[4,2048]{1,0:T(4,128)S(1)}, f32[8,128]{1,0:T(8,128)S(1)}, f32[1,2048]{1,0:T(1,128)S(1)}, f32[1,2048]{1,0:T(1,128)S(1)}, f32[1,2048]{1,0:T(1,128)S(1)}, /*index=5*/f32[1,2048]{1,0:T(1,128)S(1)}) custom-call(s32[4,2]{1,0:T(4,128)S(1)} %copy.19.partner_ref, s32[8]{0:T(128)S(1)} %bitcast.27, s32[4,2048]{1,0:T(4,128)S(1)} %bitcast.18, ...), custom_call_target="tpu_custom_call" | custom-call | flops 2000000000 | bytes 4000000 | tf_op jit(solution)/shard_map/coarse/pallas_call | solution.py:349
  143.6 4.0 %collective-permute-start.8 = (f32[1,2048]{1,0:T(1,128)S(1)}, f32[1,2048]{1,0:T(1,128)S(1)}, u32[]{:S(2)}, u32[]{:S(2)}) collective-permute-start(f32[1,2048]{1,0:T(1,128)S(1)} %get-tuple-element.53), channel_id=1, source_target_pairs={{0,8},{8,0},{16,24},{24,16},{32,40},{40,32},{48,56},{56,48},{64,72... | collective-permute-start | bytes 24584 | tf_op jit(solution)/shard_map/ppermute | solution.py:371
  147.6 2.1 %collective-permute-start.9 = (f32[1,2048]{1,0:T(1,128)S(1)}, f32[1,2048]{1,0:T(1,128)S(1)}, u32[]{:S(2)}, u32[]{:S(2)}) collective-permute-start(f32[1,2048]{1,0:T(1,128)S(1)} %get-tuple-element.54), channel_id=1, source_target_pairs={{8,16},{16,8},{24,32},{32,24},{40,48},{48,40},{56,64},{64,56},{72,... | collective-permute-start | bytes 24584 | tf_op jit(solution)/shard_map/ppermute | solution.py:372
  149.7 2.9 %collective-permute-start.10 = (f32[1,2048]{1,0:T(1,128)S(1)}, f32[1,2048]{1,0:T(1,128)S(1)}, u32[]{:S(2)}, u32[]{:S(2)}) collective-permute-start(f32[1,2048]{1,0:T(1,128)S(1)} %get-tuple-element.55), channel_id=1, source_target_pairs={{0,1},{1,0},{2,3},{3,2},{4,5},{5,4},{6,7},{7,6},{8,9},{9,8},{10,11... | collective-permute-start | bytes 24584 | tf_op jit(solution)/shard_map/ppermute | solution.py:373
  152.5 2.2 %collective-permute-start.11 = (f32[1,2048]{1,0:T(1,128)S(1)}, f32[1,2048]{1,0:T(1,128)S(1)}, u32[]{:S(2)}, u32[]{:S(2)}) collective-permute-start(f32[1,2048]{1,0:T(1,128)S(1)} %get-tuple-element.56), channel_id=1, source_target_pairs={{1,2},{2,1},{3,4},{4,3},{5,6},{6,5},{7,0},{0,7},{9,10},{10,9},{11,... | collective-permute-start | bytes 24584 | tf_op jit(solution)/shard_map/ppermute | solution.py:374
  154.8 3.3 %collective-permute-done.11.m3_ref = f32[1,2048]{1,0:T(1,128)S(1)} collective-permute-done((f32[1,2048]{1,0:T(1,128)S(1)}, f32[1,2048]{1,0:T(1,128)S(1)}, u32[]{:S(2)}, u32[]{:S(2)}) %collective-permute-start.11) | collective-permute-done | bytes 8224 | tf_op jit(solution)/shard_map/ppermute | solution.py:374
  158.1 1.7 %end.1 = (f32[4,2048]{1,0:T(4,128)}, f32[4,2048]{1,0:T(4,128)}) custom-call(s32[4,2]{1,0:T(4,128)S(1)} %copy.19.partner_ref, f32[4,2048]{1,0:T(4,128)S(1)} %get-tuple-element.51.near_ref, f32[8,128]{1,0:T(8,128)S(1)} %get-tuple-element.52.sums_ref, f32[8,128]{1,0:T(8,128)S(1)} %get-tuple-element.43.sums_ref.first_ref, ...), custom_call_target="tpu_custom_call" | custom-call | flops 1000 | bytes 4000000 | tf_op jit(solution)/shard_map/end/pallas_call | solution.py:349
  (35 shorter events, 4.9 us)
Async XLA Ops:
  7.2 77.4 %all-gather.2.cloned.1.call-start = ((), (), s32[]{:S(2)}) async-start(), calls=%async_computation.4 | async-start | bytes 2654208 | tf_op jit(solution)/shard_map/all_gather | solution.py:385
  9.3 0.9 copy-start.2
  10.2 0.8 copy-start.3
  11.1 0.8 copy-start.4
  11.8 0.7 copy-start.6
  12.5 0.7 copy-start.7
  13.2 0.7 copy-start.8
  13.9 0.7 copy-start.9
  14.6 0.7 copy-start.10
  15.3 0.7 copy-start.11
  15.9 27.0 %copy-start.5 = (s32[1,1,4,2048]{3,2,1,0:T(4,128)S(1)}, s32[1,1,4,2048]{3,2,1,0:T(4,128)}, u32[]{:S(2)}) copy-start(s32[1,1,4,2048]{3,2,1,0:T(4,128)} %param.20) | copy-start | bytes 98308
  15.9 27.0 %copy-start.12 = (s32[1,1,8]{2,1,0:T(1,128)S(1)}, s32[1,1,8]{2,1,0:T(1,128)}, u32[]{:S(2)}) copy-start(s32[1,1,8]{2,1,0:T(1,128)} %param.21) | copy-start | bytes 100
  20.5 18.2 %collective-permute-start = (f32[2,2048]{1,0:T(2,128)S(1)}, f32[2,2048]{1,0:T(2,128)S(1)}, u32[]{:S(2)}, u32[]{:S(2)}) collective-permute-start(f32[2,2048]{1,0:T(2,128)S(1)} %get-tuple-element.32), channel_id=1, source_target_pairs={{0,8},{8,0},{16,24},{24,16},{32,40},{40,32},{48,56},{56,48},{64,72... | collective-permute-start | bytes 49160 | tf_op jit(solution)/shard_map/ppermute | solution.py:371
  32.9 5.8 %collective-permute-start.1 = (f32[2,2048]{1,0:T(2,128)S(1)}, f32[2,2048]{1,0:T(2,128)S(1)}, u32[]{:S(2)}, u32[]{:S(2)}) collective-permute-start(f32[2,2048]{1,0:T(2,128)S(1)} %get-tuple-element.33), channel_id=1, source_target_pairs={{8,16},{16,8},{24,32},{32,24},{40,48},{48,40},{56,64},{64,56},{72,... | collective-permute-start | bytes 49160 | tf_op jit(solution)/shard_map/ppermute | solution.py:372
  34.9 5.2 %collective-permute-start.2 = (f32[2,2048]{1,0:T(2,128)S(1)}, f32[2,2048]{1,0:T(2,128)S(1)}, u32[]{:S(2)}, u32[]{:S(2)}) collective-permute-start(f32[2,2048]{1,0:T(2,128)S(1)} %get-tuple-element.34), channel_id=1, source_target_pairs={{0,1},{1,0},{2,3},{3,2},{4,5},{5,4},{6,7},{7,6},{8,9},{9,8},{10,11... | collective-permute-start | bytes 49160 | tf_op jit(solution)/shard_map/ppermute | solution.py:373
  36.8 6.1 %collective-permute-start.3 = (f32[2,2048]{1,0:T(2,128)S(1)}, f32[2,2048]{1,0:T(2,128)S(1)}, u32[]{:S(2)}, u32[]{:S(2)}) collective-permute-start(f32[2,2048]{1,0:T(2,128)S(1)} %get-tuple-element.35), channel_id=1, source_target_pairs={{1,2},{2,1},{3,4},{4,3},{5,6},{6,5},{7,0},{0,7},{9,10},{10,9},{11,... | collective-permute-start | bytes 49160 | tf_op jit(solution)/shard_map/ppermute | solution.py:374
  84.5 1.7 copy-start
  90.4 11.3 %collective-permute-start.4 = (f32[1,2048]{1,0:T(1,128)S(1)}, f32[1,2048]{1,0:T(1,128)S(1)}, u32[]{:S(2)}, u32[]{:S(2)}) collective-permute-start(f32[1,2048]{1,0:T(1,128)S(1)} %get-tuple-element.44), channel_id=1, source_target_pairs={{0,8},{8,0},{16,24},{24,16},{32,40},{40,32},{48,56},{56,48},{64,72... | collective-permute-start | bytes 24584 | tf_op jit(solution)/shard_map/ppermute | solution.py:371
  94.4 7.3 %collective-permute-start.5 = (f32[1,2048]{1,0:T(1,128)S(1)}, f32[1,2048]{1,0:T(1,128)S(1)}, u32[]{:S(2)}, u32[]{:S(2)}) collective-permute-start(f32[1,2048]{1,0:T(1,128)S(1)} %get-tuple-element.45), channel_id=1, source_target_pairs={{8,16},{16,8},{24,32},{32,24},{40,48},{48,40},{56,64},{64,56},{72,... | collective-permute-start | bytes 24584 | tf_op jit(solution)/shard_map/ppermute | solution.py:372
  96.6 5.2 %collective-permute-start.6 = (f32[1,2048]{1,0:T(1,128)S(1)}, f32[1,2048]{1,0:T(1,128)S(1)}, u32[]{:S(2)}, u32[]{:S(2)}) collective-permute-start(f32[1,2048]{1,0:T(1,128)S(1)} %get-tuple-element.46), channel_id=1, source_target_pairs={{0,1},{1,0},{2,3},{3,2},{4,5},{5,4},{6,7},{7,6},{8,9},{9,8},{10,11... | collective-permute-start | bytes 24584 | tf_op jit(solution)/shard_map/ppermute | solution.py:373
  99.5 5.6 %collective-permute-start.7 = (f32[1,2048]{1,0:T(1,128)S(1)}, f32[1,2048]{1,0:T(1,128)S(1)}, u32[]{:S(2)}, u32[]{:S(2)}) collective-permute-start(f32[1,2048]{1,0:T(1,128)S(1)} %get-tuple-element.47), channel_id=1, source_target_pairs={{1,2},{2,1},{3,4},{4,3},{5,6},{6,5},{7,0},{0,7},{9,10},{10,9},{11,... | collective-permute-start | bytes 24584 | tf_op jit(solution)/shard_map/ppermute | solution.py:374
  105.1 34.4 %copy-start.1 = (f32[768,768]{1,0:T(8,128)S(1)}, f32[768,768]{1,0:T(8,128)}, u32[]{:S(2)}) copy-start(f32[768,768]{1,0:T(8,128)} %all-gather.2.cloned.1.call-done.inverse_ref) | copy-start | bytes 7077892
  143.6 11.2 %collective-permute-start.8 = (f32[1,2048]{1,0:T(1,128)S(1)}, f32[1,2048]{1,0:T(1,128)S(1)}, u32[]{:S(2)}, u32[]{:S(2)}) collective-permute-start(f32[1,2048]{1,0:T(1,128)S(1)} %get-tuple-element.53), channel_id=1, source_target_pairs={{0,8},{8,0},{16,24},{24,16},{32,40},{40,32},{48,56},{56,48},{64,72... | collective-permute-start | bytes 24584 | tf_op jit(solution)/shard_map/ppermute | solution.py:371
  147.6 7.2 %collective-permute-start.9 = (f32[1,2048]{1,0:T(1,128)S(1)}, f32[1,2048]{1,0:T(1,128)S(1)}, u32[]{:S(2)}, u32[]{:S(2)}) collective-permute-start(f32[1,2048]{1,0:T(1,128)S(1)} %get-tuple-element.54), channel_id=1, source_target_pairs={{8,16},{16,8},{24,32},{32,24},{40,48},{48,40},{56,64},{64,56},{72,... | collective-permute-start | bytes 24584 | tf_op jit(solution)/shard_map/ppermute | solution.py:372
  149.7 5.1 %collective-permute-start.10 = (f32[1,2048]{1,0:T(1,128)S(1)}, f32[1,2048]{1,0:T(1,128)S(1)}, u32[]{:S(2)}, u32[]{:S(2)}) collective-permute-start(f32[1,2048]{1,0:T(1,128)S(1)} %get-tuple-element.55), channel_id=1, source_target_pairs={{0,1},{1,0},{2,3},{3,2},{4,5},{5,4},{6,7},{7,6},{8,9},{9,8},{10,11... | collective-permute-start | bytes 24584 | tf_op jit(solution)/shard_map/ppermute | solution.py:373
  152.5 5.6 %collective-permute-start.11 = (f32[1,2048]{1,0:T(1,128)S(1)}, f32[1,2048]{1,0:T(1,128)S(1)}, u32[]{:S(2)}, u32[]{:S(2)}) collective-permute-start(f32[1,2048]{1,0:T(1,128)S(1)} %get-tuple-element.56), channel_id=1, source_target_pairs={{1,2},{2,1},{3,4},{4,3},{5,6},{6,5},{7,0},{0,7},{9,10},{10,9},{11,... | collective-permute-start | bytes 24584 | tf_op jit(solution)/shard_map/ppermute | solution.py:374
Sparse Core Ops, SparseCore 0:
  10.4 51.1 all-gather.1

commit v2 on v1

v2 whole, which is shorter than its diff:
```python
import functools

import jax
import jax.numpy as jnp
import numpy as np
from jax import lax
from jax.experimental import pallas as pl
from jax.experimental.pallas import tpu as pltpu
from jax.sharding import Mesh, PartitionSpec as P

F32 = jnp.float32
BF16 = jnp.bfloat16
I32 = jnp.int32

NX, NZ, NCORE, NY = 4, 12, 2, 8
NSUB = NX * NZ * NCORE
PLANE = 256
DEPTH = 128
COLOURS = 4
WIDTH = 2048
CORNERS = 8
TOTAL = 768
CHUNK = 512
NT = (((1,), (1,)), ((), ()))
TN = (((0,), (0,)), ((), ()))


def iota(shape, dim):
    return lax.broadcasted_iota(I32, shape, dim)


def split(x):
    high = x.astype(BF16)
    return high, (x - high.astype(F32)).astype(BF16)


def dot(a, b, dims=None):
    if dims is None:
        return jnp.dot(a, b, preferred_element_type=F32)
    return lax.dot_general(a, b, dims, preferred_element_type=F32)


def dot_full(a, b, dims=(((1,), (0,)), ((), ()))):
    return lax.dot_general(a, b, dims, precision=lax.Precision.HIGHEST, preferred_element_type=F32)


def thirds(x):
    high = x.astype(BF16)
    rest = x - high.astype(F32)
    middle = rest.astype(BF16)
    return high, middle, (rest - middle.astype(F32)).astype(BF16)


def product(a, b):
    (ah, am, al), (bh, bm, bl) = a, b
    return dot(ah, bh) + ((dot(am, bh) + dot(ah, bm)) + ((dot(al, bh) + dot(am, bm)) + dot(ah, bl)))


def position():
    sub = (lax.axis_index("x") * NZ + lax.axis_index("z")) * NCORE + lax.axis_index("core")
    return sub, lax.axis_index("y")


def colour_of_links(partner_ref):
    sub, col = position()
    odd_sub, odd_col = lax.rem(sub, 2), lax.rem(col, 2)
    mates = (
        (lax.rem(sub + 2 * odd_sub - 1 + NSUB, NSUB), col),
        (sub, col + 1 - 2 * odd_col),
        (sub, lax.rem(col + 2 * odd_col - 1 + NY, NY)),
        (sub + 1 - 2 * odd_sub, col),
    )
    links = []
    for mate_sub, mate_col in mates:
        colour = jnp.int32(0)
        for c in range(1, COLOURS):
            hit = (partner_ref[0, c] == mate_sub) & (partner_ref[1, c] == mate_col)
            colour = jnp.where(hit, jnp.int32(c), colour)
        links.append(colour)
    return links


def signs(partner_ref):
    sub, col = position()
    me = sub * NY + col
    which = iota((COLOURS, WIDTH), 0)
    result = jnp.full((COLOURS, WIDTH), 1.0, F32)
    for c in range(COLOURS):
        value = jnp.where(me < partner_ref[0, c] * NY + partner_ref[1, c], 1.0, -1.0).astype(F32)
        result = jnp.where(which == c, value, result)
    return result


def by_class(classes, table_ref):
    result = jnp.full(classes.shape, table_ref[0], F32)
    for k in range(1, 16):
        result = jnp.where(classes == k, table_ref[k], result)
    return result


def level(count):
    return iota((count, CHUNK), 0).astype(F32).astype(BF16)


def one_hot(levels, row):
    return jnp.where(levels == row.astype(F32).astype(BF16), jnp.ones((), BF16), jnp.zeros((), BF16))


def gather(parts, rows_ref, outs):
    stacked = jnp.concatenate([p for group in parts for p in group], axis=0)
    counts = [len(group) for group in parts]
    planes = level(PLANE)

    for j in range(WIDTH // CHUNK):
        here = slice(j * CHUNK, (j + 1) * CHUNK)
        for c in range(COLOURS):
            node = rows_ref[c : c + 1, here]
            mask = iota((DEPTH, CHUNK), 0) == (node & 127)
            picked = dot(stacked, one_hot(planes, node >> 7))
            at = 0
            for out, count in zip(outs, counts):
                total = picked[at * DEPTH : (at + 1) * DEPTH]
                for extra in range(1, count):
                    total = total + picked[(at + extra) * DEPTH : (at + extra + 1) * DEPTH]
                at += count
                out[c : c + 1, here] = jnp.sum(jnp.where(mask, total, 0.0), axis=0, keepdims=True)


def scatter(values_ref, rows_ref):
    planes, depths = level(PLANE), level(DEPTH)
    total = jnp.zeros((2 * DEPTH, PLANE), F32)
    for j in range(WIDTH // CHUNK):
        here = slice(j * CHUNK, (j + 1) * CHUNK)
        for c in range(COLOURS):
            node = rows_ref[c : c + 1, here]
            mask = depths == (node & 127).astype(F32).astype(BF16)
            parts = split(values_ref[c : c + 1, here])
            left = jnp.concatenate([jnp.where(mask, part, jnp.zeros_like(part)) for part in parts], axis=0)
            total = total + dot(left, one_hot(planes, node >> 7), NT)
    return total[:DEPTH] + total[DEPTH:]


def forward(field, planes, depths):
    return product(depths[3:], thirds(product(thirds(field), planes[:3])))


def backward(spectrum, planes, depths):
    return product(depths[:3], thirds(product(thirds(spectrum), planes[3:])))


def kernel_start(
    mode_x_hbm, mode_y_hbm, mode_z_hbm, eigen_hbm, classes_hbm, loads_hbm, rows_hbm, partner_hbm, corner_hbm, coef_hbm,
    planes_ref, depths_ref, fields_ref, corners_ref, rows_ref, near_ref, m0_ref, m1_ref, m2_ref, m3_ref,
    cls_ref, mode_x_ref, mode_y_ref, mode_z_ref, eigen_ref, classes_ref, loads_ref, partner_ref, corner_ref, coef_ref,
    sems,
):
    copies = []
    for i, (source, target) in enumerate((
        (mode_x_hbm, mode_x_ref), (mode_y_hbm, mode_y_ref), (mode_z_hbm, mode_z_ref), (eigen_hbm, eigen_ref),
        (classes_hbm, classes_ref), (loads_hbm, loads_ref), (rows_hbm, rows_ref), (partner_hbm, partner_ref),
        (corner_hbm, corner_ref), (coef_hbm, coef_ref),
    )):
        copies.append(pltpu.make_async_copy(source, target, sems.at[i]))
        copies[-1].start()
    copies[0].wait()
    copies[1].wait()
    spread_x = (iota((16, PLANE), 0) == (iota((16, PLANE), 1) >> 4)).astype(F32)
    spread_y = (iota((16, PLANE), 0) == (iota((16, PLANE), 1) & 15)).astype(F32)
    wide_x = dot_full(mode_x_ref[...], spread_x)
    wide_y = dot_full(mode_y_ref[...], spread_y)
    tall_x = dot_full(mode_x_ref[...], spread_x, TN)
    tall_y = dot_full(mode_y_ref[...], spread_y, TN)
    for i in range(16):
        here = slice(16 * i, 16 * i + 16)
        for k, part in enumerate(thirds(wide_x[i : i + 1] * wide_y) + thirds(tall_x[i : i + 1] * tall_y)):
            planes_ref[k, here] = part
    copies[2].wait()
    mode_z = mode_z_ref[...]
    for k, part in enumerate(thirds(mode_z) + thirds(mode_z.T)):
        depths_ref[k] = part
    planes = [planes_ref[i] for i in range(6)]
    depths = [depths_ref[i] for i in range(6)]

    copies[3].wait()
    line = dot_full(eigen_ref[:, 0:16], spread_x) + dot_full(eigen_ref[:, 16:32], spread_y)
    diagonal = iota((DEPTH, DEPTH), 0) == iota((DEPTH, DEPTH), 1)
    column = jnp.sum(jnp.where(diagonal, eigen_ref[:, 32:160], 0.0), axis=1, keepdims=True)
    lam_inv = 1.0 / (line + column)
    fields_ref[0] = lam_inv

    copies[4].wait()
    copies[8].wait()
    copies[9].wait()
    spread_c = (iota((16, PLANE), 0) == ((iota((16, PLANE), 1) >> 6) * 4 + ((iota((16, PLANE), 1) >> 2) & 3))).astype(BF16)
    spread_d = (iota((DEPTH, 32), 1) == (iota((DEPTH, 32), 0) >> 2)).astype(BF16)
    small = classes_ref[...].astype(F32).astype(BF16)
    deep = dot(spread_d, small, NT).astype(BF16)
    node_class = dot(deep, spread_c)
    class_part = node_class.astype(BF16)
    root = 1.0 / jnp.sqrt(by_class(node_class.astype(I32), coef_ref))
    fields_ref[1] = root

    node = jnp.zeros((CORNERS, 1), I32)
    for t in range(CORNERS):
        node = jnp.where(iota((CORNERS, 1), 0) == t, corner_ref[t], node)
    hot_plane = (iota((CORNERS, PLANE), 1) == (node >> 7)).astype(F32)
    hot_depth = (iota((CORNERS, DEPTH), 1) == (node & 127)).astype(F32)
    hot_p, hot_d = hot_plane.astype(BF16), hot_depth.astype(BF16)
    corner_class = jnp.sum(dot(hot_d, class_part) * hot_plane, axis=1, keepdims=True)
    corner_root = 1.0 / jnp.sqrt(by_class(corner_class.astype(I32), coef_ref))
    corners_ref[0:8, :] = dot(hot_p, planes[0]) + (dot(hot_p, planes[1]) + dot(hot_p, planes[2]))
    corners_ref[8:16, 0:DEPTH] = (dot(hot_d, depths[0]) + (dot(hot_d, depths[1]) + dot(hot_d, depths[2]))) * corner_root
    corners_ref[8:16, DEPTH:] = jnp.zeros((8, PLANE - DEPTH), F32)

    copies[5].wait()
    copies[6].wait()
    copies[7].wait()
    weights = forward(loads_ref[...].T * root, planes, depths) * lam_inv
    high, low = split(backward(weights, planes, depths) * root)
    gather([(high, low), (class_part,)], rows_ref, [near_ref.at[0], cls_ref])
    near_ref[1] = by_class(cls_ref[...].astype(I32), coef_ref)
    for link, message in zip(colour_of_links(partner_ref), (m0_ref, m1_ref, m2_ref, m3_ref)):
        message[0:1, :] = near_ref[0, pl.ds(link, 1), :]
        message[1:2, :] = near_ref[1, pl.ds(link, 1), :]


def reduce_all(x):
    return jnp.sum(jnp.sum(x, axis=1, keepdims=True), axis=0, keepdims=True)


def launch(ids_ref, rows_ref, x_ref, planes, depths, fields_ref, corners_ref, extras, weights_ref, send_ref):
    lam_inv, root = fields_ref[0], fields_ref[1]
    modes = forward(scatter(x_ref, rows_ref) * root, planes, depths)
    weights = modes * lam_inv
    weights_ref[...] = weights
    energy = reduce_all(weights * modes)
    part = dot_full(corners_ref[0:8, :], weights, NT) * corners_ref[8:16, 0:DEPTH]
    part = jnp.sum(part, axis=1, keepdims=True)
    lane = iota((1, 128), 1)
    row = jnp.zeros((1, 128), F32)
    for t in range(CORNERS):
        row = jnp.where(lane == t, part[t : t + 1, 0:1], row)
        row = jnp.where(lane == CORNERS + t, ids_ref[t].astype(F32), row)
    for at, scalar in enumerate([energy] + extras):
        row = jnp.where(lane == 2 * CORNERS + at, scalar, row)
    send_ref[...] = jnp.broadcast_to(row, send_ref.shape)


def receive(partner_ref, messages, far_ref):
    count = messages[0].shape[0]
    for link, message in zip(colour_of_links(partner_ref), messages):
        for i in range(count):
            far_ref[i, pl.ds(link, 1), :] = message[i : i + 1, :]


def kernel_first(
    partner_ref, ids_ref, rows_ref, near_ref, m0_ref, m1_ref, m2_ref, m3_ref,
    planes_ref, depths_ref, fields_ref, corners_ref,
    state_ref, weights_ref, send_ref,
    far_ref, x_ref,
):
    receive(partner_ref, (m0_ref, m1_ref, m2_ref, m3_ref), far_ref)
    sign = signs(partner_ref)
    a, a_far = near_ref[1], far_ref[1]
    rhs = sign * (near_ref[0] - far_ref[0])
    weight = a * a_far / (a + a_far)
    precond = weight * rhs
    state_ref[0] = rhs
    state_ref[1] = weight
    x_ref[...] = sign * precond
    planes = [planes_ref[i] for i in range(6)]
    depths = [depths_ref[i] for i in range(6)]
    launch(
        ids_ref, rows_ref, x_ref, planes, depths, fields_ref, corners_ref, [reduce_all(rhs * precond)],
        weights_ref, send_ref,
    )


def kernel_relay(got_ref, send_ref):
    got = got_ref[...]
    count = got.shape[0]
    spot = iota((count, TOTAL), 1).astype(F32)
    line = jnp.zeros((count, TOTAL), F32)
    for t in range(CORNERS):
        line = line + jnp.where(spot == got[:, CORNERS + t : CORNERS + t + 1], got[:, t : t + 1], 0.0)
    line = jnp.sum(jnp.concatenate([line, got], axis=1), axis=0, keepdims=True)
    send_ref[...] = jnp.broadcast_to(line, send_ref.shape)


def kernel_coarse(
    partner_ref, ids_ref, rows_ref, got_ref, inverse_ref, weights_ref,
    planes_ref, depths_ref, fields_ref, corners_ref,
    near_ref, sums_ref, m0_ref, m1_ref, m2_ref, m3_ref,
):
    got = jnp.sum(got_ref[...], axis=0, keepdims=True)
    line = got[:, :TOTAL]
    high = line.astype(BF16).astype(F32)
    middle = (line - high).astype(BF16).astype(F32)
    low = line - high - middle
    which = iota((8, TOTAL), 0)
    left = jnp.where(which == 0, high, jnp.where(which == 1, middle, jnp.where(which == 2, low, 0.0))).astype(BF16)
    inverse_high, inverse_low = split(inverse_ref[...])
    coarse = jnp.sum(dot(left, inverse_high) + dot(left, inverse_low), axis=0, keepdims=True)
    work = reduce_all(coarse * line)
    first = 2 * CORNERS
    sums_ref[...] = jnp.where(iota((8, 128), 1) == first + 3, work, jnp.broadcast_to(got[:, TOTAL:], (8, 128)))
    ids = jnp.zeros((CORNERS, 1), I32)
    for t in range(CORNERS):
        ids = jnp.where(iota((CORNERS, 1), 0) == t, ids_ref[t], ids)
    own = jnp.sum(jnp.where(iota((CORNERS, TOTAL), 1) == ids, coarse, 0.0), axis=1, keepdims=True)
    lam_inv, root = fields_ref[0], fields_ref[1]
    lifted = dot_full(corners_ref[8:16, 0:DEPTH] * own, corners_ref[0:8, :], TN)
    weights = weights_ref[...] + lam_inv * lifted
    planes = [planes_ref[i] for i in range(6)]
    depths = [depths_ref[i] for i in range(6)]
    high, low = split(backward(weights, planes, depths) * root)
    gather([(high, low)], rows_ref, [near_ref])
    for link, message in zip(colour_of_links(partner_ref), (m0_ref, m1_ref, m2_ref, m3_ref)):
        message[...] = near_ref[pl.ds(link, 1), :]


def scalars_of(sums_ref):
    return (sums_ref[0:1, i : i + 1] for i in range(2 * CORNERS, 2 * CORNERS + 4))


def kernel_second(
    partner_ref, ids_ref, rows_ref, near_ref, sums_ref, m0_ref, m1_ref, m2_ref, m3_ref, state_ref,
    planes_ref, depths_ref, fields_ref, corners_ref,
    later_ref, weights_ref, send_ref,
    far_ref, x_ref,
):
    receive(partner_ref, (m0_ref, m1_ref, m2_ref, m3_ref), far_ref)
    sign = signs(partner_ref)
    image = sign * (near_ref[...] - far_ref[0])
    energy, rz, _, work = scalars_of(sums_ref)
    alpha = rz / (2.0 * (energy + work))
    rhs, weight = state_ref[0], state_ref[1]
    residual = rhs - alpha * image
    precond = weight * residual
    later_ref[0] = image
    later_ref[1] = residual
    later_ref[2] = precond
    later_ref[3] = weight * rhs
    x_ref[...] = sign * precond
    planes = [planes_ref[i] for i in range(6)]
    depths = [depths_ref[i] for i in range(6)]
    launch(
        ids_ref, rows_ref, x_ref, planes, depths, fields_ref, corners_ref,
        [reduce_all(residual * precond), reduce_all(precond * image)], weights_ref, send_ref,
    )


def kernel_end(
    partner_ref, near_ref, sums_ref, first_ref, m0_ref, m1_ref, m2_ref, m3_ref, later_ref,
    multipliers_ref, residual_ref,
    far_ref,
):
    receive(partner_ref, (m0_ref, m1_ref, m2_ref, m3_ref), far_ref)
    sign = signs(partner_ref)
    energy, rz, _, work = scalars_of(first_ref)
    form = 2.0 * (energy + work)
    alpha = rz / form
    energy, rz_next, cross, work = scalars_of(sums_ref)
    beta = rz_next / rz
    form_next = 2.0 * (energy + work) + beta * (2.0 * cross + beta * form)
    alpha_next = rz_next / form_next
    image, residual, precond, direction = (later_ref[i] for i in range(4))
    image_next = sign * (near_ref[...] - far_ref[0]) + beta * image
    direction_next = precond + beta * direction
    multipliers_ref[...] = alpha * direction + alpha_next * direction_next
    residual_ref[...] = residual - alpha_next * image_next


VMEM = pl.BlockSpec(memory_space=pltpu.VMEM)
SMEM = pl.BlockSpec(memory_space=pltpu.SMEM)
HBM = pl.BlockSpec(memory_space=pltpu.HBM)


def call(kernel, name, scalars, arrays, outs, scratch=(), flops=2_000_000_000, space=VMEM):
    if space is HBM:
        arrays = [pltpu.with_memory_space_constraint(a, pltpu.HBM) for a in arrays]
    return pl.pallas_call(
        kernel,
        name=name,
        out_shape=[jax.ShapeDtypeStruct(*o) for o in outs],
        in_specs=[SMEM] * len(scalars) + [space] * len(arrays),
        out_specs=[VMEM] * len(outs),
        scratch_shapes=[pltpu.VMEM(*s) if isinstance(s, tuple) else s for s in scratch],
        compiler_params=pltpu.CompilerParams(vmem_limit_bytes=40 * 1024 * 1024),
        cost_estimate=pl.CostEstimate(flops=flops, bytes_accessed=4_000_000, transcendentals=0),
    )(*scalars, *arrays)


def pairing(size, first):
    pairs = []
    for i in range(first, size + first, 2):
        a, b = i % size, (i + 1) % size
        pairs += [(a, b), (b, a)]
    return pairs


def exchange(messages):
    sub = ("x", "z", "core")
    far_sub = lax.ppermute(messages[0], sub, pairing(NSUB, 1))
    near_col = lax.ppermute(messages[1], "y", pairing(NY, 0))
    far_col = lax.ppermute(messages[2], "y", pairing(NY, 1))
    mate = lax.ppermute(messages[3], sub, pairing(NSUB, 0))
    return far_sub, near_col, far_col, mate


def on_device(
    loads, mode_x, mode_y, mode_z, eigen, classes, coefficients, partner, rows, corner_id, corner_row, coarse_inverse
):
    inverse = lax.all_gather(coarse_inverse, "y", axis=0, tiled=True)
    partner = partner[0, 0].T
    ids = corner_id[0, 0]
    halo = (2, WIDTH)
    one = (1, WIDTH)
    wide = (COLOURS, WIDTH)
    planes, depths, fields, corners, rows, near, *messages = call(
        kernel_start,
        "start",
        [],
        [
            mode_x[0, 0], mode_y[0, 0], mode_z[0, 0], eigen[0], classes.reshape(16, 32),
            loads.reshape(PLANE, DEPTH), rows[0, 0], partner, corner_row[0, 0], coefficients,
        ],
        [
            ((6, PLANE, PLANE), BF16), ((6, DEPTH, DEPTH), BF16), ((2, DEPTH, PLANE), F32), ((16, PLANE), F32),
            (wide, I32), ((2, *wide), F32), (halo, F32), (halo, F32), (halo, F32), (halo, F32),
        ],
        [
            (wide, F32), ((16, 16), F32), ((16, 16), F32), ((DEPTH, DEPTH), F32), ((1, 160), F32), ((16, 32), I32),
            ((PLANE, DEPTH), F32), pltpu.SMEM((2, COLOURS), I32), pltpu.SMEM((CORNERS,), I32), pltpu.SMEM((16,), F32),
            pltpu.SemaphoreType.DMA((10,)),
        ],
        space=HBM,
    )
    shared = [planes, depths, fields, corners]
    messages = exchange(messages)

    def total(send):
        got = lax.all_to_all(send, ("z", "core"), 0, 0, tiled=True)
        (send,) = call(kernel_relay, "relay", [], [got], [((NX * NY, TOTAL + 128), F32)], flops=1000)
        return lax.all_to_all(send, ("x", "y"), 0, 0, tiled=True)

    weights_out = ((DEPTH, PLANE), F32)
    send_out = ((NZ * NCORE, 128), F32)
    scratch = [((2, *wide), F32), (wide, F32)]
    state, weights, send = call(
        kernel_first, "first", [partner, ids], [rows, near, *messages, *shared],
        [((2, *wide), F32), weights_out, send_out], scratch,
    )
    coarse_outs = [(wide, F32), ((8, 128), F32), (one, F32), (one, F32), (one, F32), (one, F32)]
    got = total(send)
    near, first_sums, *messages = call(
        kernel_coarse, "coarse", [partner, ids], [rows, got, inverse, weights, *shared], coarse_outs
    )
    messages = exchange(messages)
    later, weights, send = call(
        kernel_second, "second", [partner, ids], [rows, near, first_sums, *messages, state, *shared],
        [((4, *wide), F32), weights_out, send_out], scratch,
    )
    got = total(send)
    near, sums, *messages = call(
        kernel_coarse, "coarse", [partner, ids], [rows, got, inverse, weights, *shared], coarse_outs
    )
    messages = exchange(messages)
    multipliers, residual = call(
        kernel_end, "end", [partner], [near, sums, first_sums, *messages, later], [(wide, F32), (wide, F32)],
        scratch[:1], flops=1000,
    )
    return multipliers[None, None], residual[None, None]


def solution(mesh):
    fine = Mesh(np.asarray(mesh.devices).reshape(NX, NZ, NCORE, NY), ("x", "z", "core", "y"))
    sub = ("x", "z", "core")
    placed = (
        P(sub, "y", None, None, None),
        P(sub, "y", None, None),
        P(sub, "y", None, None),
        P(sub, "y", None, None),
        P(sub, "y", None),
        P(sub, "y", None, None, None),
        P(),
        P(sub, "y", None, None),
        P(sub, "y", None, None),
        P(sub, "y", None),
        P(sub, "y", None),
        P("y", None),
    )
    return jax.shard_map(
        on_device,
        mesh=fine,
        in_specs=placed,
        out_specs=(P(sub, "y", None, None), P(sub, "y", None, None)),
        check_vma=False,
    )
```

time: 169 us -> 149 us (0.88)
  blocking collectives: 68 us -> 56.2 us
  starting transfers between devices: 40.7 us -> 51.2 us
  waiting for transfers between devices: 11.6 us -> 3.49 us
  local copies, waits for them, and re-layouts: 9.68 us -> 1.93 us
    all_to_all x4, blocking collectives: 68 us -> 56.2 us  [the longest x2 29.6 us: total(): return lax.all_to_all(send, ('x', 'y'), 0, 0, tiled=True)]
    ppermute x12, starting transfers between devices: 40.6 us -> 51.2 us  [the longest x3 19.5 us: exchange(): mate = lax.ppermute(messages[3], sub, pairing(NSUB, 0))]
    ppermute x12, waiting for transfers between devices: 10.9 us -> 2.78 us  [the longest x3 1.98 us: exchange(): far_col = lax.ppermute(messages[2], 'y', pairing(NY, 1))]
    unnamed x26 -> x10, local copies, waits for them, and re-layouts: 8.25 us -> 1.69 us
  transfers between devices with their start and end apart: 13 -> 13, of which waited for: 4 -> 3; matrix products, arithmetic and copies ran while one was open for 1% -> 0% of each run, Pallas kernels for 5% -> 6%
where the time goes in v2:
time: 149 us; the launch traced here: 148 us
  blocking collectives  56.2 us (38%)
  starting transfers between devices  51.2 us (34%)
  Pallas kernels  21.2 us (14%)
  between operations  14.3 us (10%)
  waiting for transfers between devices  3.49 us (2%)
  local copies, waits for them, and re-layouts  1.93 us (1%)
    all_to_all x2, blocking collectives, total(): return lax.all_to_all(send, ('x', 'y'), 0, 0, tiled=True)  29.6 us
    all_to_all x2, blocking collectives, total(): got = lax.all_to_all(send, ('z', 'core'), 0, 0, tiled=True)  26.5 us
    pallas_call x8, Pallas kernels, call(): pl.pallas_call(kernel, name=name, out_shape=[jax.ShapeDtypeStruct(*o) for...  21.2 us
    ppermute x3, starting transfers between devices, exchange(): mate = lax.ppermute(messages[3], sub, pairing(NSUB, 0))  19.5 us
    ppermute x3, starting transfers between devices, exchange(): far_sub = lax.ppermute(messages[0], sub, pairing(NSUB, 1))  13.6 us
    ppermute x3, starting transfers between devices, exchange(): far_col = lax.ppermute(messages[2], 'y', pairing(NY, 1))  9.37 us
    ppermute x3, starting transfers between devices, exchange(): near_col = lax.ppermute(messages[1], 'y', pairing(NY, 0))  8.77 us
  transfers between devices with their start and end apart: 13, of which 3 were waited for; matrix products, arithmetic and copies ran while one was open for 0% of the time, Pallas kernels for 6%

profile of v2, /device:TPU:1, one launch (start us, length us, event | category | flops | bytes accessed | tf_op | source)
XLA Modules:
  0.0 148.3 jit_solution(9437793146064037135)
XLA Ops:
  7.2 0.0 all-gather.2.cloned.1.call-start
  7.2 0.7 all-gather.2.cloned.1.call-update
  7.9 5.5 %start.1 = (bf16[6,256,256]{2,1,0:T(8,128)(2,1)S(1)}, bf16[6,128,128]{2,1,0:T(8,128)(2,1)S(1)}, f32[2,128,256]{2,1,0:T(8,128)S(1)}, f32[16,256]{1,0:T(8,128)S(1)...) custom-call(f32[16,16]{1,0:T(8,128)} %bitcast.53, ...), custom_call_target="tpu_custom_call" | custom-call | flops 2000000000 | bytes 4000000 | tf_op jit(solution)/shard_map/start/pallas_call | solution.py:382
  13.5 5.4 %collective-permute-start = (f32[2,2048]{1,0:T(2,128)S(1)}, f32[2,2048]{1,0:T(2,128)S(1)}, u32[]{:S(2)}, u32[]{:S(2)}) collective-permute-start(f32[2,2048]{1,0:T(2,128)S(1)} %get-tuple-element.34), channel_id=1, source_target_pairs={{8,16},{16,8},{24,32},{32,24},{40,48},{48,40},{56,64},{64,56},{72,... | collective-permute-start | bytes 49160 | tf_op jit(solution)/shard_map/ppermute | solution.py:404
  18.9 3.2 %collective-permute-start.1 = (f32[2,2048]{1,0:T(2,128)S(1)}, f32[2,2048]{1,0:T(2,128)S(1)}, u32[]{:S(2)}, u32[]{:S(2)}) collective-permute-start(f32[2,2048]{1,0:T(2,128)S(1)} %get-tuple-element.35), channel_id=1, source_target_pairs={{0,1},{1,0},{2,3},{3,2},{4,5},{5,4},{6,7},{7,6},{8,9},{9,8},{10,11... | collective-permute-start | bytes 49160 | tf_op jit(solution)/shard_map/ppermute | solution.py:405
  22.1 4.9 %collective-permute-start.2 = (f32[2,2048]{1,0:T(2,128)S(1)}, f32[2,2048]{1,0:T(2,128)S(1)}, u32[]{:S(2)}, u32[]{:S(2)}) collective-permute-start(f32[2,2048]{1,0:T(2,128)S(1)} %get-tuple-element.36), channel_id=1, source_target_pairs={{1,2},{2,1},{3,4},{4,3},{5,6},{6,5},{7,0},{0,7},{9,10},{10,9},{11,... | collective-permute-start | bytes 49160 | tf_op jit(solution)/shard_map/ppermute | solution.py:406
  26.9 14.8 %collective-permute-start.3 = (f32[2,2048]{1,0:T(2,128)S(1)}, f32[2,2048]{1,0:T(2,128)S(1)}, u32[]{:S(2)}, u32[]{:S(2)}) collective-permute-start(f32[2,2048]{1,0:T(2,128)S(1)} %get-tuple-element.37), channel_id=1, source_target_pairs={{0,8},{8,0},{16,24},{24,16},{32,40},{40,32},{48,56},{56,48},{64,72... | collective-permute-start | bytes 49160 | tf_op jit(solution)/shard_map/ppermute | solution.py:407
  41.8 0.8 collective-permute-done.3.m3_ref
  42.6 3.2 %first.1 = (f32[2,4,2048]{2,1,0:T(4,128)S(1)}, f32[128,256]{1,0:T(8,128)S(1)}, f32[24,128]{1,0:T(8,128)S(1)}) custom-call(s32[2,4]{1,0:T(2,128)S(1)} %bitcast.39, s32[8]{0:T(128)S(1)} %bitcast.44, s32[4,2048]{1,0:T(4,128)S(1)} %get-tuple-element.32.rows_ref, f32[2,4,2048]{2,1,0:T(4,128)S(1)} %get-tuple-element.33.near_ref, ...), custom_call_target="tpu_custom_call" | custom-call | flops 2000000000 | bytes 4000000 | tf_op jit(solution)/shard_map/first/pallas_call | solution.py:382
  45.7 12.6 %all_to_all.44 = f32[24,1,128]{2,1,0:T(1,128)S(1)} all-to-all(f32[24,1,128]{2,1,0:T(1,128)S(1)} %bitcast.37), channel_id=1, replica_groups=mesh['x'=4,'z'=12,'core'=2,'y'=8] {'z','core'}, dimensions={0} | all-to-all | bytes 24576 | tf_op jit(solution)/shard_map/all_to_all | solution.py:443
  58.3 0.2 relay.2
  58.5 0.1 copy.15
  58.6 14.4 %all_to_all.45 = f32[32,1,896]{2,1,0:T(1,128)S(1)} all-to-all(f32[32,1,896]{2,1,0:T(1,128)S(1)} %copy.15), channel_id=1, replica_groups=mesh['x'=4,'z'=12,'core'=2,'y'=8] {'x','y'}, dimensions={0} | all-to-all | bytes 229376 | tf_op jit(solution)/shard_map/all_to_all | solution.py:445
  73.0 1.7 %copy-done.1 = f32[768,768]{1,0:T(8,128)S(1)} copy-done((f32[768,768]{1,0:T(8,128)S(1)}, f32[768,768]{1,0:T(8,128)}, u32[]{:S(2)}) %copy-start.1) | copy-done | bytes 2359320
  74.7 3.6 %coarse.2 = (f32[4,2048]{1,0:T(4,128)S(1)}, f32[8,128]{1,0:T(8,128)S(1)}, f32[1,2048]{1,0:T(1,128)S(1)}, f32[1,2048]{1,0:T(1,128)S(1)}, f32[1,2048]{1,0:T(1,128)S(1)}, /*index=5*/f32[1,2048]{1,0:T(1,128)S(1)}) custom-call(s32[2,4]{1,0:T(2,128)S(1)} %bitcast.40, s32[8]{0:T(128)S(1)} %bitcast.45, s32[4,2048]{1,0:T(4,128)S(1)} %get-tuple-element.32.rows_ref, ...), custom_call_target="tpu_custom_call" | custom-call | flops 2000000000 | bytes 4000000 | tf_op jit(solution)/shard_map/coarse/pallas_call | solution.py:382
  78.3 4.1 %collective-permute-start.4 = (f32[1,2048]{1,0:T(1,128)S(1)}, f32[1,2048]{1,0:T(1,128)S(1)}, u32[]{:S(2)}, u32[]{:S(2)}) collective-permute-start(f32[1,2048]{1,0:T(1,128)S(1)} %get-tuple-element.46), channel_id=1, source_target_pairs={{8,16},{16,8},{24,32},{32,24},{40,48},{48,40},{56,64},{64,56},{72,... | collective-permute-start | bytes 24584 | tf_op jit(solution)/shard_map/ppermute | solution.py:404
  82.3 2.8 %collective-permute-start.5 = (f32[1,2048]{1,0:T(1,128)S(1)}, f32[1,2048]{1,0:T(1,128)S(1)}, u32[]{:S(2)}, u32[]{:S(2)}) collective-permute-start(f32[1,2048]{1,0:T(1,128)S(1)} %get-tuple-element.47), channel_id=1, source_target_pairs={{0,1},{1,0},{2,3},{3,2},{4,5},{5,4},{6,7},{7,6},{8,9},{9,8},{10,11... | collective-permute-start | bytes 24584 | tf_op jit(solution)/shard_map/ppermute | solution.py:405
  85.1 2.3 %collective-permute-start.6 = (f32[1,2048]{1,0:T(1,128)S(1)}, f32[1,2048]{1,0:T(1,128)S(1)}, u32[]{:S(2)}, u32[]{:S(2)}) collective-permute-start(f32[1,2048]{1,0:T(1,128)S(1)} %get-tuple-element.48), channel_id=1, source_target_pairs={{1,2},{2,1},{3,4},{4,3},{5,6},{6,5},{7,0},{0,7},{9,10},{10,9},{11,... | collective-permute-start | bytes 24584 | tf_op jit(solution)/shard_map/ppermute | solution.py:406
  87.4 2.4 %collective-permute-start.7 = (f32[1,2048]{1,0:T(1,128)S(1)}, f32[1,2048]{1,0:T(1,128)S(1)}, u32[]{:S(2)}, u32[]{:S(2)}) collective-permute-start(f32[1,2048]{1,0:T(1,128)S(1)} %get-tuple-element.49), channel_id=1, source_target_pairs={{0,8},{8,0},{16,24},{24,16},{32,40},{40,32},{48,56},{56,48},{64,72... | collective-permute-start | bytes 24584 | tf_op jit(solution)/shard_map/ppermute | solution.py:407
  89.8 1.0 collective-permute-done.6.m2_ref
  90.7 3.3 %second.1 = (f32[4,4,2048]{2,1,0:T(4,128)S(1)}, f32[128,256]{1,0:T(8,128)S(1)}, f32[24,128]{1,0:T(8,128)S(1)}) custom-call(s32[2,4]{1,0:T(2,128)S(1)} %bitcast.41, s32[8]{0:T(128)S(1)} %bitcast.46, s32[4,2048]{1,0:T(4,128)S(1)} %get-tuple-element.32.rows_ref, f32[4,2048]{1,0:T(4,128)S(1)} %get-tuple-element.44.near_ref, ...), custom_call_target="tpu_custom_call" | custom-call | flops 2000000000 | bytes 4000000 | tf_op jit(solution)/shard_map/second/pallas_call | solution.py:382
  94.1 14.0 %all_to_all.46 = f32[24,1,128]{2,1,0:T(1,128)S(1)} all-to-all(f32[24,1,128]{2,1,0:T(1,128)S(1)} %bitcast.36), channel_id=1, replica_groups=mesh['x'=4,'z'=12,'core'=2,'y'=8] {'z','core'}, dimensions={0} | all-to-all | bytes 24576 | tf_op jit(solution)/shard_map/all_to_all | solution.py:443
  108.1 0.2 relay.3
  108.2 0.1 copy.17
  108.3 15.2 %all_to_all.47 = f32[32,1,896]{2,1,0:T(1,128)S(1)} all-to-all(f32[32,1,896]{2,1,0:T(1,128)S(1)} %copy.17), channel_id=1, replica_groups=mesh['x'=4,'z'=12,'core'=2,'y'=8] {'x','y'}, dimensions={0} | all-to-all | bytes 229376 | tf_op jit(solution)/shard_map/all_to_all | solution.py:445
  123.6 3.6 %coarse.3 = (f32[4,2048]{1,0:T(4,128)S(1)}, f32[8,128]{1,0:T(8,128)S(1)}, f32[1,2048]{1,0:T(1,128)S(1)}, f32[1,2048]{1,0:T(1,128)S(1)}, f32[1,2048]{1,0:T(1,128)S(1)}, /*index=5*/f32[1,2048]{1,0:T(1,128)S(1)}) custom-call(s32[2,4]{1,0:T(2,128)S(1)} %bitcast.42, s32[8]{0:T(128)S(1)} %bitcast.47, s32[4,2048]{1,0:T(4,128)S(1)} %get-tuple-element.32.rows_ref, ...), custom_call_target="tpu_custom_call" | custom-call | flops 2000000000 | bytes 4000000 | tf_op jit(solution)/shard_map/coarse/pallas_call | solution.py:382
  127.2 4.1 %collective-permute-start.8 = (f32[1,2048]{1,0:T(1,128)S(1)}, f32[1,2048]{1,0:T(1,128)S(1)}, u32[]{:S(2)}, u32[]{:S(2)}) collective-permute-start(f32[1,2048]{1,0:T(1,128)S(1)} %get-tuple-element.55), channel_id=1, source_target_pairs={{8,16},{16,8},{24,32},{32,24},{40,48},{48,40},{56,64},{64,56},{72,... | collective-permute-start | bytes 24584 | tf_op jit(solution)/shard_map/ppermute | solution.py:404
  131.3 2.8 %collective-permute-start.9 = (f32[1,2048]{1,0:T(1,128)S(1)}, f32[1,2048]{1,0:T(1,128)S(1)}, u32[]{:S(2)}, u32[]{:S(2)}) collective-permute-start(f32[1,2048]{1,0:T(1,128)S(1)} %get-tuple-element.56), channel_id=1, source_target_pairs={{0,1},{1,0},{2,3},{3,2},{4,5},{5,4},{6,7},{7,6},{8,9},{9,8},{10,11... | collective-permute-start | bytes 24584 | tf_op jit(solution)/shard_map/ppermute | solution.py:405
  134.1 2.2 %collective-permute-start.10 = (f32[1,2048]{1,0:T(1,128)S(1)}, f32[1,2048]{1,0:T(1,128)S(1)}, u32[]{:S(2)}, u32[]{:S(2)}) collective-permute-start(f32[1,2048]{1,0:T(1,128)S(1)} %get-tuple-element.57), channel_id=1, source_target_pairs={{1,2},{2,1},{3,4},{4,3},{5,6},{6,5},{7,0},{0,7},{9,10},{10,9},{11,... | collective-permute-start | bytes 24584 | tf_op jit(solution)/shard_map/ppermute | solution.py:406
  136.4 2.3 %collective-permute-start.11 = (f32[1,2048]{1,0:T(1,128)S(1)}, f32[1,2048]{1,0:T(1,128)S(1)}, u32[]{:S(2)}, u32[]{:S(2)}) collective-permute-start(f32[1,2048]{1,0:T(1,128)S(1)} %get-tuple-element.58), channel_id=1, source_target_pairs={{0,8},{8,0},{16,24},{24,16},{32,40},{40,32},{48,56},{56,48},{64,72... | collective-permute-start | bytes 24584 | tf_op jit(solution)/shard_map/ppermute | solution.py:407
  138.7 1.0 collective-permute-done.10.m2_ref
  139.8 1.7 %end.1 = (f32[4,2048]{1,0:T(4,128)}, f32[4,2048]{1,0:T(4,128)}) custom-call(s32[2,4]{1,0:T(2,128)S(1)} %bitcast.43, f32[4,2048]{1,0:T(4,128)S(1)} %get-tuple-element.53.near_ref, f32[8,128]{1,0:T(8,128)S(1)} %get-tuple-element.54.sums_ref, f32[8,128]{1,0:T(8,128)S(1)} %get-tuple-element.45.sums_ref.first_ref, f32[1,2048]{1,0:T(1,128)S(1)} %collective-permute-done.8.m0_ref, ...), custom_call_target="tpu_custom_call" | custom-call | flops 1000 | bytes 4000000 | tf_op jit(solution)/shard_map/end/pallas_call | solution.py:382
  (19 shorter events, 0.1 us)
Async XLA Ops:
  7.2 65.9 %all-gather.2.cloned.1.call-start = ((), (), s32[]{:S(2)}) async-start(), calls=%async_computation.4 | async-start | bytes 2654208 | tf_op jit(solution)/shard_map/all_gather | solution.py:414
  7.9 34.7 %copy-start = (s32[1,1,4,2]{2,3,1,0:T(2,128)S(1)}, s32[1,1,4,2]{2,3,1,0:T(2,128)}, u32[]{:S(2)}) copy-start(s32[1,1,4,2]{2,3,1,0:T(2,128)} %param.19) | copy-start | bytes 100
  7.9 34.7 %copy-start.3 = (s32[1,1,8]{2,1,0:T(1,128)S(1)}, s32[1,1,8]{2,1,0:T(1,128)}, u32[]{:S(2)}) copy-start(s32[1,1,8]{2,1,0:T(1,128)} %param.21) | copy-start | bytes 100
  13.5 28.3 %collective-permute-start = (f32[2,2048]{1,0:T(2,128)S(1)}, f32[2,2048]{1,0:T(2,128)S(1)}, u32[]{:S(2)}, u32[]{:S(2)}) collective-permute-start(f32[2,2048]{1,0:T(2,128)S(1)} %get-tuple-element.34), channel_id=1, source_target_pairs={{8,16},{16,8},{24,32},{32,24},{40,48},{48,40},{56,64},{64,56},{72,... | collective-permute-start | bytes 49160 | tf_op jit(solution)/shard_map/ppermute | solution.py:404
  18.9 22.9 %collective-permute-start.1 = (f32[2,2048]{1,0:T(2,128)S(1)}, f32[2,2048]{1,0:T(2,128)S(1)}, u32[]{:S(2)}, u32[]{:S(2)}) collective-permute-start(f32[2,2048]{1,0:T(2,128)S(1)} %get-tuple-element.35), channel_id=1, source_target_pairs={{0,1},{1,0},{2,3},{3,2},{4,5},{5,4},{6,7},{7,6},{8,9},{9,8},{10,11... | collective-permute-start | bytes 49160 | tf_op jit(solution)/shard_map/ppermute | solution.py:405
  22.1 19.7 %collective-permute-start.2 = (f32[2,2048]{1,0:T(2,128)S(1)}, f32[2,2048]{1,0:T(2,128)S(1)}, u32[]{:S(2)}, u32[]{:S(2)}) collective-permute-start(f32[2,2048]{1,0:T(2,128)S(1)} %get-tuple-element.36), channel_id=1, source_target_pairs={{1,2},{2,1},{3,4},{4,3},{5,6},{6,5},{7,0},{0,7},{9,10},{10,9},{11,... | collective-permute-start | bytes 49160 | tf_op jit(solution)/shard_map/ppermute | solution.py:406
  26.9 15.6 %collective-permute-start.3 = (f32[2,2048]{1,0:T(2,128)S(1)}, f32[2,2048]{1,0:T(2,128)S(1)}, u32[]{:S(2)}, u32[]{:S(2)}) collective-permute-start(f32[2,2048]{1,0:T(2,128)S(1)} %get-tuple-element.37), channel_id=1, source_target_pairs={{0,8},{8,0},{16,24},{24,16},{32,40},{40,32},{48,56},{56,48},{64,72... | collective-permute-start | bytes 49160 | tf_op jit(solution)/shard_map/ppermute | solution.py:407
  73.0 1.7 %copy-start.1 = (f32[768,768]{1,0:T(8,128)S(1)}, f32[768,768]{1,0:T(8,128)}, u32[]{:S(2)}) copy-start(f32[768,768]{1,0:T(8,128)} %all-gather.2.cloned.1.call-done.inverse_ref) | copy-start | bytes 7077892
  78.3 11.5 %collective-permute-start.4 = (f32[1,2048]{1,0:T(1,128)S(1)}, f32[1,2048]{1,0:T(1,128)S(1)}, u32[]{:S(2)}, u32[]{:S(2)}) collective-permute-start(f32[1,2048]{1,0:T(1,128)S(1)} %get-tuple-element.46), channel_id=1, source_target_pairs={{8,16},{16,8},{24,32},{32,24},{40,48},{48,40},{56,64},{64,56},{72,... | collective-permute-start | bytes 24584 | tf_op jit(solution)/shard_map/ppermute | solution.py:404
  82.3 7.4 %collective-permute-start.5 = (f32[1,2048]{1,0:T(1,128)S(1)}, f32[1,2048]{1,0:T(1,128)S(1)}, u32[]{:S(2)}, u32[]{:S(2)}) collective-permute-start(f32[1,2048]{1,0:T(1,128)S(1)} %get-tuple-element.47), channel_id=1, source_target_pairs={{0,1},{1,0},{2,3},{3,2},{4,5},{5,4},{6,7},{7,6},{8,9},{9,8},{10,11... | collective-permute-start | bytes 24584 | tf_op jit(solution)/shard_map/ppermute | solution.py:405
  85.1 5.6 %collective-permute-start.6 = (f32[1,2048]{1,0:T(1,128)S(1)}, f32[1,2048]{1,0:T(1,128)S(1)}, u32[]{:S(2)}, u32[]{:S(2)}) collective-permute-start(f32[1,2048]{1,0:T(1,128)S(1)} %get-tuple-element.48), channel_id=1, source_target_pairs={{1,2},{2,1},{3,4},{4,3},{5,6},{6,5},{7,0},{0,7},{9,10},{10,9},{11,... | collective-permute-start | bytes 24584 | tf_op jit(solution)/shard_map/ppermute | solution.py:406
  87.4 3.3 %collective-permute-start.7 = (f32[1,2048]{1,0:T(1,128)S(1)}, f32[1,2048]{1,0:T(1,128)S(1)}, u32[]{:S(2)}, u32[]{:S(2)}) collective-permute-start(f32[1,2048]{1,0:T(1,128)S(1)} %get-tuple-element.49), channel_id=1, source_target_pairs={{0,8},{8,0},{16,24},{24,16},{32,40},{40,32},{48,56},{56,48},{64,72... | collective-permute-start | bytes 24584 | tf_op jit(solution)/shard_map/ppermute | solution.py:407
  90.7 32.9 %copy-start.2 = (f32[768,768]{1,0:T(8,128)S(1)}, f32[768,768]{1,0:T(8,128)}, u32[]{:S(2)}) copy-start(f32[768,768]{1,0:T(8,128)} %all-gather.2.cloned.1.call-done.inverse_ref) | copy-start | bytes 7077892
  127.2 11.5 %collective-permute-start.8 = (f32[1,2048]{1,0:T(1,128)S(1)}, f32[1,2048]{1,0:T(1,128)S(1)}, u32[]{:S(2)}, u32[]{:S(2)}) collective-permute-start(f32[1,2048]{1,0:T(1,128)S(1)} %get-tuple-element.55), channel_id=1, source_target_pairs={{8,16},{16,8},{24,32},{32,24},{40,48},{48,40},{56,64},{64,56},{72,... | collective-permute-start | bytes 24584 | tf_op jit(solution)/shard_map/ppermute | solution.py:404
  131.3 7.4 %collective-permute-start.9 = (f32[1,2048]{1,0:T(1,128)S(1)}, f32[1,2048]{1,0:T(1,128)S(1)}, u32[]{:S(2)}, u32[]{:S(2)}) collective-permute-start(f32[1,2048]{1,0:T(1,128)S(1)} %get-tuple-element.56), channel_id=1, source_target_pairs={{0,1},{1,0},{2,3},{3,2},{4,5},{5,4},{6,7},{7,6},{8,9},{9,8},{10,11... | collective-permute-start | bytes 24584 | tf_op jit(solution)/shard_map/ppermute | solution.py:405
  134.1 5.6 %collective-permute-start.10 = (f32[1,2048]{1,0:T(1,128)S(1)}, f32[1,2048]{1,0:T(1,128)S(1)}, u32[]{:S(2)}, u32[]{:S(2)}) collective-permute-start(f32[1,2048]{1,0:T(1,128)S(1)} %get-tuple-element.57), channel_id=1, source_target_pairs={{1,2},{2,1},{3,4},{4,3},{5,6},{6,5},{7,0},{0,7},{9,10},{10,9},{11,... | collective-permute-start | bytes 24584 | tf_op jit(solution)/shard_map/ppermute | solution.py:406
  136.4 3.4 %collective-permute-start.11 = (f32[1,2048]{1,0:T(1,128)S(1)}, f32[1,2048]{1,0:T(1,128)S(1)}, u32[]{:S(2)}, u32[]{:S(2)}) collective-permute-start(f32[1,2048]{1,0:T(1,128)S(1)} %get-tuple-element.58), channel_id=1, source_target_pairs={{0,8},{8,0},{16,24},{24,16},{32,40},{40,32},{48,56},{56,48},{64,72... | collective-permute-start | bytes 24584 | tf_op jit(solution)/shard_map/ppermute | solution.py:407
Sparse Core Ops, SparseCore 0:
  10.4 51.3 all-gather.1

commit v3 on v2

--- a/solution.py
+++ b/solution.py
@@ -20,6 +20,7 @@
 WIDTH = 2048
 CORNERS = 8
 TOTAL = 768
+SHARES = 4
 CHUNK = 512
 NT = (((1,), (1,)), ((), ()))
 TN = (((0,), (0,)), ((), ()))
@@ -59,6 +60,10 @@
 def position():
     sub = (lax.axis_index("x") * NZ + lax.axis_index("z")) * NCORE + lax.axis_index("core")
     return sub, lax.axis_index("y")
+
+
+def share():
+    return lax.rem(lax.axis_index("x"), 2) * NCORE + lax.axis_index("core")
 
 
 def colour_of_links(partner_ref):
@@ -288,7 +293,7 @@
 
 
 def kernel_coarse(
-    partner_ref, ids_ref, rows_ref, got_ref, inverse_ref, weights_ref,
+    partner_ref, ids_ref, rows_ref, got_ref, own_ref, side_ref, mate_ref, weights_ref,
     planes_ref, depths_ref, fields_ref, corners_ref,
     near_ref, sums_ref, m0_ref, m1_ref, m2_ref, m3_ref,
 ):
@@ -298,18 +303,33 @@
     middle = (line - high).astype(BF16).astype(F32)
     low = line - high - middle
     which = iota((8, TOTAL), 0)
-    left = jnp.where(which == 0, high, jnp.where(which == 1, middle, jnp.where(which == 2, low, 0.0))).astype(BF16)
-    inverse_high, inverse_low = split(inverse_ref[...])
-    coarse = jnp.sum(dot(left, inverse_high) + dot(left, inverse_low), axis=0, keepdims=True)
+    left = jnp.where(which == 0, high, jnp.where(which == 1, middle, jnp.where(which == 2, low, 0.0)))
+    coarse = jnp.zeros((8, TOTAL), F32)
+    part = TOTAL // NY // SHARES
+    lefts = [
+        jnp.concatenate([left[:, (SHARES * i + q) * part : (SHARES * i + q + 1) * part] for i in range(NY)], axis=1)
+        for q in range(SHARES)
+    ]
+    mine = share()
+    half = NY * part
+    blocks = (own_ref[...], side_ref[...], mate_ref[0:half, :], mate_ref[half:, :])
+    for flip, block in zip((0, 2, 1, 3), blocks):
+        chosen = lefts[flip]
+        for q in range(1, SHARES):
+            chosen = jnp.where(mine == q, lefts[q ^ flip], chosen)
+        chosen = chosen.astype(BF16)
+        block_high, block_low = split(block)
+        coarse = coarse + (dot(chosen, block_high) + dot(chosen, block_low))
+    coarse = jnp.sum(coarse, axis=0, keepdims=True)
     work = reduce_all(coarse * line)
     first = 2 * CORNERS
     sums_ref[...] = jnp.where(iota((8, 128), 1) == first + 3, work, jnp.broadcast_to(got[:, TOTAL:], (8, 128)))
     ids = jnp.zeros((CORNERS, 1), I32)
     for t in range(CORNERS):
         ids = jnp.where(iota((CORNERS, 1), 0) == t, ids_ref[t], ids)
-    own = jnp.sum(jnp.where(iota((CORNERS, TOTAL), 1) == ids, coarse, 0.0), axis=1, keepdims=True)
+    at_ids = jnp.sum(jnp.where(iota((CORNERS, TOTAL), 1) == ids, coarse, 0.0), axis=1, keepdims=True)
     lam_inv, root = fields_ref[0], fields_ref[1]
-    lifted = dot_full(corners_ref[8:16, 0:DEPTH] * own, corners_ref[0:8, :], TN)
+    lifted = dot_full(corners_ref[8:16, 0:DEPTH] * at_ids, corners_ref[0:8, :], TN)
     weights = weights_ref[...] + lam_inv * lifted
     planes = [planes_ref[i] for i in range(6)]
     depths = [depths_ref[i] for i in range(6)]
@@ -411,7 +431,10 @@
 def on_device(
     loads, mode_x, mode_y, mode_z, eigen, classes, coefficients, partner, rows, corner_id, corner_row, coarse_inverse
 ):
-    inverse = lax.all_gather(coarse_inverse, "y", axis=0, tiled=True)
+    part = coarse_inverse.shape[0] // SHARES
+    quarter = lax.dynamic_slice(coarse_inverse, (share() * part, 0), (part, TOTAL))
+    quarter = jnp.broadcast_to(quarter[None], (NY, part, TOTAL)).reshape(NY * part, TOTAL)
+    own = lax.all_to_all(quarter, "y", 0, 0, tiled=True)
     partner = partner[0, 0].T
     ids = corner_id[0, 0]
     halo = (2, WIDTH)
@@ -438,11 +461,14 @@
     )
     shared = [planes, depths, fields, corners]
     messages = exchange(messages)
-
-    def total(send):
+    messages, own = lax.optimization_barrier((messages, own))
+    side = lax.ppermute(own, "x", pairing(NX, 0))
+
+    def total(send, held):
         got = lax.all_to_all(send, ("z", "core"), 0, 0, tiled=True)
+        got, held = lax.optimization_barrier((got, held))
         (send,) = call(kernel_relay, "relay", [], [got], [((NX * NY, TOTAL + 128), F32)], flops=1000)
-        return lax.all_to_all(send, ("x", "y"), 0, 0, tiled=True)
+        return lax.all_to_all(send, ("x", "y"), 0, 0, tiled=True), held
 
     weights_out = ((DEPTH, PLANE), F32)
     send_out = ((NZ * NCORE, 128), F32)
@@ -452,18 +478,19 @@
         [((2, *wide), F32), weights_out, send_out], scratch,
     )
     coarse_outs = [(wide, F32), ((8, 128), F32), (one, F32), (one, F32), (one, F32), (one, F32)]
-    got = total(send)
+    got, (own, side) = total(send, (own, side))
+    mate = lax.ppermute(jnp.concatenate([own, side], axis=0), ("x", "z", "core"), pairing(NSUB, 0))
     near, first_sums, *messages = call(
-        kernel_coarse, "coarse", [partner, ids], [rows, got, inverse, weights, *shared], coarse_outs
+        kernel_coarse, "coarse", [partner, ids], [rows, got, own, side, mate, weights, *shared], coarse_outs
     )
     messages = exchange(messages)
     later, weights, send = call(
         kernel_second, "second", [partner, ids], [rows, near, first_sums, *messages, state, *shared],
         [((4, *wide), F32), weights_out, send_out], scratch,
     )
-    got = total(send)
+    got, _ = total(send, ())
     near, sums, *messages = call(
-        kernel_coarse, "coarse", [partner, ids], [rows, got, inverse, weights, *shared], coarse_outs
+        kernel_coarse, "coarse", [partner, ids], [rows, got, own, side, mate, weights, *shared], coarse_outs
     )
     messages = exchange(messages)
     multipliers, residual = call(

time: 149 us -> 148 us (level)
  between operations: 14.3 us -> 0.92 us
  starting transfers between devices: 51.2 us -> 62.3 us
    all_to_all x0 -> x1, starting transfers between devices: none -> 7.65 us  [on_device(): own = lax.all_to_all(quarter, 'y', 0, 0, tiled=True)]
    ppermute x0 -> x2, starting transfers between devices: none -> 4.47 us  [the longest x1 2.57 us: on_device(): lax.ppermute(jnp.concatenate([own, side], axis=0), ('x', 'z', 'core'), pa...]
  transfers between devices with their start and end apart: 13 -> 15, of which waited for: 3 -> 4; matrix products, arithmetic and copies ran while one was open for 0% -> 0% of each run, Pallas kernels for 6% -> 6%
where the time goes in v3:
time: 148 us; the launch traced here: 147 us
  starting transfers between devices  62.3 us (42%)
  blocking collectives  57.5 us (39%)
  Pallas kernels  21.3 us (14%)
  waiting for transfers between devices  2.62 us (2%)
  local copies, waits for them, and re-layouts  2.08 us (1%)
    all_to_all x2, blocking collectives, total(): return (lax.all_to_all(send, ('x', 'y'), 0, 0, tiled=True), held)  30.4 us
    all_to_all x2, blocking collectives, total(): got = lax.all_to_all(send, ('z', 'core'), 0, 0, tiled=True)  27.1 us
    pallas_call x8, Pallas kernels, call(): pl.pallas_call(kernel, name=name, out_shape=[jax.ShapeDtypeStruct(*o) for...  21.3 us
    ppermute x3, starting transfers between devices, exchange(): mate = lax.ppermute(messages[3], sub, pairing(NSUB, 0))  19.2 us
    ppermute x3, starting transfers between devices, exchange(): far_sub = lax.ppermute(messages[0], sub, pairing(NSUB, 1))  12.9 us
    ppermute x3, starting transfers between devices, exchange(): near_col = lax.ppermute(messages[1], 'y', pairing(NY, 0))  9.17 us
    ppermute x3, starting transfers between devices, exchange(): far_col = lax.ppermute(messages[2], 'y', pairing(NY, 1))  8.82 us
    all_to_all x1, starting transfers between devices, on_device(): own = lax.all_to_all(quarter, 'y', 0, 0, tiled=True)  7.65 us
  transfers between devices with their start and end apart: 15, of which 4 were waited for; matrix products, arithmetic and copies ran while one was open for 0% of the time, Pallas kernels for 6%

profile of v3, /device:TPU:1, one launch (start us, length us, event | category | flops | bytes accessed | tf_op | source)
XLA Modules:
  0.0 146.8 jit_solution(3564059992178450662)
XLA Ops:
  0.7 0.9 copy-done
  1.6 0.9 broadcast_in_dim.12
  2.5 7.7 %all-to-all-start = ((f32[8,24,768]{2,1,0:T(8,128)}), f32[8,24,768]{2,1,0:T(8,128)S(1)}, u32[]{:S(2)}, u32[]{:S(2)}) async-start(f32[8,24,768]{2,1,0:T(8,128)} %broadcast_in_dim.12), calls=%async_computation | async-start | bytes 1179648 | tf_op jit(solution)/shard_map/all_to_all | solution.py:437
  10.1 5.5 %start.1 = (bf16[6,256,256]{2,1,0:T(8,128)(2,1)S(1)}, bf16[6,128,128]{2,1,0:T(8,128)(2,1)S(1)}, f32[2,128,256]{2,1,0:T(8,128)S(1)}, f32[16,256]{1,0:T(8,128)S(1)...) custom-call(f32[16,16]{1,0:T(8,128)} %bitcast.58, ...), custom_call_target="tpu_custom_call" | custom-call | flops 2000000000 | bytes 4000000 | tf_op jit(solution)/shard_map/start/pallas_call | solution.py:402
  15.7 4.8 %collective-permute-start = (f32[2,2048]{1,0:T(2,128)S(1)}, f32[2,2048]{1,0:T(2,128)S(1)}, u32[]{:S(2)}, u32[]{:S(2)}) collective-permute-start(f32[2,2048]{1,0:T(2,128)S(1)} %get-tuple-element.42), channel_id=1, source_target_pairs={{8,16},{16,8},{24,32},{32,24},{40,48},{48,40},{56,64},{64,56},{72,... | collective-permute-start | bytes 49160 | tf_op jit(solution)/shard_map/ppermute | solution.py:424
  20.5 3.6 %collective-permute-start.1 = (f32[2,2048]{1,0:T(2,128)S(1)}, f32[2,2048]{1,0:T(2,128)S(1)}, u32[]{:S(2)}, u32[]{:S(2)}) collective-permute-start(f32[2,2048]{1,0:T(2,128)S(1)} %get-tuple-element.43), channel_id=1, source_target_pairs={{0,1},{1,0},{2,3},{3,2},{4,5},{5,4},{6,7},{7,6},{8,9},{9,8},{10,11... | collective-permute-start | bytes 49160 | tf_op jit(solution)/shard_map/ppermute | solution.py:425
  24.2 4.3 %collective-permute-start.2 = (f32[2,2048]{1,0:T(2,128)S(1)}, f32[2,2048]{1,0:T(2,128)S(1)}, u32[]{:S(2)}, u32[]{:S(2)}) collective-permute-start(f32[2,2048]{1,0:T(2,128)S(1)} %get-tuple-element.44), channel_id=1, source_target_pairs={{1,2},{2,1},{3,4},{4,3},{5,6},{6,5},{7,0},{0,7},{9,10},{10,9},{11,... | collective-permute-start | bytes 49160 | tf_op jit(solution)/shard_map/ppermute | solution.py:426
  28.5 14.2 %collective-permute-start.3 = (f32[2,2048]{1,0:T(2,128)S(1)}, f32[2,2048]{1,0:T(2,128)S(1)}, u32[]{:S(2)}, u32[]{:S(2)}) collective-permute-start(f32[2,2048]{1,0:T(2,128)S(1)} %get-tuple-element.45), channel_id=1, source_target_pairs={{0,8},{8,0},{16,24},{24,16},{32,40},{40,32},{48,56},{56,48},{64,72... | collective-permute-start | bytes 49160 | tf_op jit(solution)/shard_map/ppermute | solution.py:427
  42.8 0.8 collective-permute-done.3.m3_ref
  43.6 1.9 %collective-permute-start.4 = (f32[192,768]{1,0:T(8,128)S(1)}, f32[192,768]{1,0:T(8,128)S(1)}, u32[]{:S(2)}, u32[]{:S(2)}) collective-permute-start(f32[192,768]{1,0:T(8,128)S(1)} %bitcast.31), channel_id=1, source_target_pairs={{0,192},{192,0},{384,576},{576,384},{1,193},{193,1},{385,577},{577... | collective-permute-start | bytes 1769480 | tf_op jit(solution)/shard_map/ppermute | solution.py:465
  45.5 3.2 %first.1 = (f32[2,4,2048]{2,1,0:T(4,128)S(1)}, f32[128,256]{1,0:T(8,128)S(1)}, f32[24,128]{1,0:T(8,128)S(1)}) custom-call(s32[2,4]{1,0:T(2,128)S(1)} %bitcast.44, s32[8]{0:T(128)S(1)} %bitcast.49, s32[4,2048]{1,0:T(4,128)S(1)} %get-tuple-element.40.rows_ref, f32[2,4,2048]{2,1,0:T(4,128)S(1)} %get-tuple-element.41.near_ref, ...), custom_call_target="tpu_custom_call" | custom-call | flops 2000000000 | bytes 4000000 | tf_op jit(solution)/shard_map/first/pallas_call | solution.py:402
  48.7 13.1 %all_to_all.55 = f32[24,1,128]{2,1,0:T(1,128)S(1)} all-to-all(f32[24,1,128]{2,1,0:T(1,128)S(1)} %bitcast.42), channel_id=1, replica_groups=mesh['x'=4,'z'=12,'core'=2,'y'=8] {'z','core'}, dimensions={0} | all-to-all | bytes 24576 | tf_op jit(solution)/shard_map/all_to_all | solution.py:468
  61.9 2.6 %collective-permute-start.5 = (f32[384,768]{1,0:T(8,128)S(1)}, f32[384,768]{1,0:T(8,128)S(1)}, u32[]{:S(2)}, u32[]{:S(2)}) collective-permute-start(f32[384,768]{1,0:T(8,128)S(1)} %pad_maximum_fusion), channel_id=1, source_target_pairs={{0,8},{8,0},{16,24},{24,16},{32,40},{40,32},{48,56},{56,48},{64,72... | collective-permute-start | bytes 3538952 | tf_op jit(solution)/shard_map/ppermute | solution.py:482
  64.5 0.2 relay.2
  64.8 15.4 %all_to_all.56 = f32[32,1,896]{2,1,0:T(1,128)S(1)} all-to-all(f32[32,1,896]{2,1,0:T(1,128)S(1)} %copy.15), channel_id=1, replica_groups=mesh['x'=4,'z'=12,'core'=2,'y'=8] {'x','y'}, dimensions={0} | all-to-all | bytes 229376 | tf_op jit(solution)/shard_map/all_to_all | solution.py:471
  80.2 3.6 %coarse.2 = (f32[4,2048]{1,0:T(4,128)S(1)}, f32[8,128]{1,0:T(8,128)S(1)}, f32[1,2048]{1,0:T(1,128)S(1)}, f32[1,2048]{1,0:T(1,128)S(1)}, f32[1,2048]{1,0:T(1,128)S(1)}, /*index=5*/f32[1,2048]{1,0:T(1,128)S(1)}) custom-call(s32[2,4]{1,0:T(2,128)S(1)} %bitcast.45, s32[8]{0:T(128)S(1)} %bitcast.50, s32[4,2048]{1,0:T(4,128)S(1)} %get-tuple-element.40.rows_ref, ...), custom_call_target="tpu_custom_call" | custom-call | flops 2000000000 | bytes 4000000 | tf_op jit(solution)/shard_map/coarse/pallas_call | solution.py:402
  83.8 4.0 %collective-permute-start.6 = (f32[1,2048]{1,0:T(1,128)S(1)}, f32[1,2048]{1,0:T(1,128)S(1)}, u32[]{:S(2)}, u32[]{:S(2)}) collective-permute-start(f32[1,2048]{1,0:T(1,128)S(1)} %get-tuple-element.62), channel_id=1, source_target_pairs={{8,16},{16,8},{24,32},{32,24},{40,48},{48,40},{56,64},{64,56},{72,... | collective-permute-start | bytes 24584 | tf_op jit(solution)/shard_map/ppermute | solution.py:424
  87.8 2.7 %collective-permute-start.7 = (f32[1,2048]{1,0:T(1,128)S(1)}, f32[1,2048]{1,0:T(1,128)S(1)}, u32[]{:S(2)}, u32[]{:S(2)}) collective-permute-start(f32[1,2048]{1,0:T(1,128)S(1)} %get-tuple-element.63), channel_id=1, source_target_pairs={{0,1},{1,0},{2,3},{3,2},{4,5},{5,4},{6,7},{7,6},{8,9},{9,8},{10,11... | collective-permute-start | bytes 24584 | tf_op jit(solution)/shard_map/ppermute | solution.py:425
  90.6 2.3 %collective-permute-start.8 = (f32[1,2048]{1,0:T(1,128)S(1)}, f32[1,2048]{1,0:T(1,128)S(1)}, u32[]{:S(2)}, u32[]{:S(2)}) collective-permute-start(f32[1,2048]{1,0:T(1,128)S(1)} %get-tuple-element.64), channel_id=1, source_target_pairs={{1,2},{2,1},{3,4},{4,3},{5,6},{6,5},{7,0},{0,7},{9,10},{10,9},{11,... | collective-permute-start | bytes 24584 | tf_op jit(solution)/shard_map/ppermute | solution.py:426
  92.9 2.7 %collective-permute-start.9 = (f32[1,2048]{1,0:T(1,128)S(1)}, f32[1,2048]{1,0:T(1,128)S(1)}, u32[]{:S(2)}, u32[]{:S(2)}) collective-permute-start(f32[1,2048]{1,0:T(1,128)S(1)} %get-tuple-element.65), channel_id=1, source_target_pairs={{0,8},{8,0},{16,24},{24,16},{32,40},{40,32},{48,56},{56,48},{64,72... | collective-permute-start | bytes 24584 | tf_op jit(solution)/shard_map/ppermute | solution.py:427
  95.5 0.6 collective-permute-done.8.m2_ref
  96.3 3.3 %second.1 = (f32[4,4,2048]{2,1,0:T(4,128)S(1)}, f32[128,256]{1,0:T(8,128)S(1)}, f32[24,128]{1,0:T(8,128)S(1)}) custom-call(s32[2,4]{1,0:T(2,128)S(1)} %bitcast.46, s32[8]{0:T(128)S(1)} %bitcast.51, s32[4,2048]{1,0:T(4,128)S(1)} %get-tuple-element.40.rows_ref, f32[4,2048]{1,0:T(4,128)S(1)} %get-tuple-element.60.near_ref, ...), custom_call_target="tpu_custom_call" | custom-call | flops 2000000000 | bytes 4000000 | tf_op jit(solution)/shard_map/second/pallas_call | solution.py:402
  99.7 14.0 %all_to_all.57 = f32[24,1,128]{2,1,0:T(1,128)S(1)} all-to-all(f32[24,1,128]{2,1,0:T(1,128)S(1)} %bitcast.41), channel_id=1, replica_groups=mesh['x'=4,'z'=12,'core'=2,'y'=8] {'z','core'}, dimensions={0} | all-to-all | bytes 24576 | tf_op jit(solution)/shard_map/all_to_all | solution.py:468
  113.7 0.2 relay.3
  114.0 15.0 %all_to_all.58 = f32[32,1,896]{2,1,0:T(1,128)S(1)} all-to-all(f32[32,1,896]{2,1,0:T(1,128)S(1)} %copy.17), channel_id=1, replica_groups=mesh['x'=4,'z'=12,'core'=2,'y'=8] {'x','y'}, dimensions={0} | all-to-all | bytes 229376 | tf_op jit(solution)/shard_map/all_to_all | solution.py:471
  129.0 3.6 %coarse.3 = (f32[4,2048]{1,0:T(4,128)S(1)}, f32[8,128]{1,0:T(8,128)S(1)}, f32[1,2048]{1,0:T(1,128)S(1)}, f32[1,2048]{1,0:T(1,128)S(1)}, f32[1,2048]{1,0:T(1,128)S(1)}, /*index=5*/f32[1,2048]{1,0:T(1,128)S(1)}) custom-call(s32[2,4]{1,0:T(2,128)S(1)} %bitcast.47, s32[8]{0:T(128)S(1)} %bitcast.52, s32[4,2048]{1,0:T(4,128)S(1)} %get-tuple-element.40.rows_ref, ...), custom_call_target="tpu_custom_call" | custom-call | flops 2000000000 | bytes 4000000 | tf_op jit(solution)/shard_map/coarse/pallas_call | solution.py:402
  132.6 4.1 %collective-permute-start.10 = (f32[1,2048]{1,0:T(1,128)S(1)}, f32[1,2048]{1,0:T(1,128)S(1)}, u32[]{:S(2)}, u32[]{:S(2)}) collective-permute-start(f32[1,2048]{1,0:T(1,128)S(1)} %get-tuple-element.71), channel_id=1, source_target_pairs={{8,16},{16,8},{24,32},{32,24},{40,48},{48,40},{56,64},{64,56},{72,... | collective-permute-start | bytes 24584 | tf_op jit(solution)/shard_map/ppermute | solution.py:424
  136.7 2.8 %collective-permute-start.11 = (f32[1,2048]{1,0:T(1,128)S(1)}, f32[1,2048]{1,0:T(1,128)S(1)}, u32[]{:S(2)}, u32[]{:S(2)}) collective-permute-start(f32[1,2048]{1,0:T(1,128)S(1)} %get-tuple-element.72), channel_id=1, source_target_pairs={{0,1},{1,0},{2,3},{3,2},{4,5},{5,4},{6,7},{7,6},{8,9},{9,8},{10,11... | collective-permute-start | bytes 24584 | tf_op jit(solution)/shard_map/ppermute | solution.py:425
  139.5 2.2 %collective-permute-start.12 = (f32[1,2048]{1,0:T(1,128)S(1)}, f32[1,2048]{1,0:T(1,128)S(1)}, u32[]{:S(2)}, u32[]{:S(2)}) collective-permute-start(f32[1,2048]{1,0:T(1,128)S(1)} %get-tuple-element.73), channel_id=1, source_target_pairs={{1,2},{2,1},{3,4},{4,3},{5,6},{6,5},{7,0},{0,7},{9,10},{10,9},{11,... | collective-permute-start | bytes 24584 | tf_op jit(solution)/shard_map/ppermute | solution.py:426
  141.8 2.3 %collective-permute-start.13 = (f32[1,2048]{1,0:T(1,128)S(1)}, f32[1,2048]{1,0:T(1,128)S(1)}, u32[]{:S(2)}, u32[]{:S(2)}) collective-permute-start(f32[1,2048]{1,0:T(1,128)S(1)} %get-tuple-element.74), channel_id=1, source_target_pairs={{0,8},{8,0},{16,24},{24,16},{32,40},{40,32},{48,56},{56,48},{64,72... | collective-permute-start | bytes 24584 | tf_op jit(solution)/shard_map/ppermute | solution.py:427
  144.1 1.0 collective-permute-done.12.m2_ref
  145.1 1.7 %end.1 = (f32[4,2048]{1,0:T(4,128)}, f32[4,2048]{1,0:T(4,128)}) custom-call(s32[2,4]{1,0:T(2,128)S(1)} %bitcast.48, f32[4,2048]{1,0:T(4,128)S(1)} %get-tuple-element.69.near_ref, f32[8,128]{1,0:T(8,128)S(1)} %get-tuple-element.70.sums_ref, f32[8,128]{1,0:T(8,128)S(1)} %get-tuple-element.61.sums_ref.first_ref, f32[1,2048]{1,0:T(1,128)S(1)} %collective-permute-done.10.m0_ref, ...), custom_call_target="tpu_custom_call" | custom-call | flops 1000 | bytes 4000000 | tf_op jit(solution)/shard_map/end/pallas_call | solution.py:402
  (23 shorter events, 0.5 us)
Async XLA Ops:
  0.6 1.0 copy-start
  2.5 41.1 %all-to-all-start = ((f32[8,24,768]{2,1,0:T(8,128)}), f32[8,24,768]{2,1,0:T(8,128)S(1)}, u32[]{:S(2)}, u32[]{:S(2)}) async-start(f32[8,24,768]{2,1,0:T(8,128)} %broadcast_in_dim.12), calls=%async_computation | async-start | bytes 1179648 | tf_op jit(solution)/shard_map/all_to_all | solution.py:437
  10.1 35.4 %copy-start.1 = (s32[1,1,4,2]{2,3,1,0:T(2,128)S(1)}, s32[1,1,4,2]{2,3,1,0:T(2,128)}, u32[]{:S(2)}) copy-start(s32[1,1,4,2]{2,3,1,0:T(2,128)} %param.19) | copy-start | bytes 100
  10.1 35.4 %copy-start.2 = (s32[1,1,8]{2,1,0:T(1,128)S(1)}, s32[1,1,8]{2,1,0:T(1,128)}, u32[]{:S(2)}) copy-start(s32[1,1,8]{2,1,0:T(1,128)} %param.21) | copy-start | bytes 100
  15.7 27.1 %collective-permute-start = (f32[2,2048]{1,0:T(2,128)S(1)}, f32[2,2048]{1,0:T(2,128)S(1)}, u32[]{:S(2)}, u32[]{:S(2)}) collective-permute-start(f32[2,2048]{1,0:T(2,128)S(1)} %get-tuple-element.42), channel_id=1, source_target_pairs={{8,16},{16,8},{24,32},{32,24},{40,48},{48,40},{56,64},{64,56},{72,... | collective-permute-start | bytes 49160 | tf_op jit(solution)/shard_map/ppermute | solution.py:424
  20.5 22.2 %collective-permute-start.1 = (f32[2,2048]{1,0:T(2,128)S(1)}, f32[2,2048]{1,0:T(2,128)S(1)}, u32[]{:S(2)}, u32[]{:S(2)}) collective-permute-start(f32[2,2048]{1,0:T(2,128)S(1)} %get-tuple-element.43), channel_id=1, source_target_pairs={{0,1},{1,0},{2,3},{3,2},{4,5},{5,4},{6,7},{7,6},{8,9},{9,8},{10,11... | collective-permute-start | bytes 49160 | tf_op jit(solution)/shard_map/ppermute | solution.py:425
  24.2 18.6 %collective-permute-start.2 = (f32[2,2048]{1,0:T(2,128)S(1)}, f32[2,2048]{1,0:T(2,128)S(1)}, u32[]{:S(2)}, u32[]{:S(2)}) collective-permute-start(f32[2,2048]{1,0:T(2,128)S(1)} %get-tuple-element.44), channel_id=1, source_target_pairs={{1,2},{2,1},{3,4},{4,3},{5,6},{6,5},{7,0},{0,7},{9,10},{10,9},{11,... | collective-permute-start | bytes 49160 | tf_op jit(solution)/shard_map/ppermute | solution.py:426
  28.5 15.1 %collective-permute-start.3 = (f32[2,2048]{1,0:T(2,128)S(1)}, f32[2,2048]{1,0:T(2,128)S(1)}, u32[]{:S(2)}, u32[]{:S(2)}) collective-permute-start(f32[2,2048]{1,0:T(2,128)S(1)} %get-tuple-element.45), channel_id=1, source_target_pairs={{0,8},{8,0},{16,24},{24,16},{32,40},{40,32},{48,56},{56,48},{64,72... | collective-permute-start | bytes 49160 | tf_op jit(solution)/shard_map/ppermute | solution.py:427
  43.6 18.3 %collective-permute-start.4 = (f32[192,768]{1,0:T(8,128)S(1)}, f32[192,768]{1,0:T(8,128)S(1)}, u32[]{:S(2)}, u32[]{:S(2)}) collective-permute-start(f32[192,768]{1,0:T(8,128)S(1)} %bitcast.31), channel_id=1, source_target_pairs={{0,192},{192,0},{384,576},{576,384},{1,193},{193,1},{385,577},{577... | collective-permute-start | bytes 1769480 | tf_op jit(solution)/shard_map/ppermute | solution.py:465
  61.9 18.3 %collective-permute-start.5 = (f32[384,768]{1,0:T(8,128)S(1)}, f32[384,768]{1,0:T(8,128)S(1)}, u32[]{:S(2)}, u32[]{:S(2)}) collective-permute-start(f32[384,768]{1,0:T(8,128)S(1)} %pad_maximum_fusion), channel_id=1, source_target_pairs={{0,8},{8,0},{16,24},{24,16},{32,40},{40,32},{48,56},{56,48},{64,72... | collective-permute-start | bytes 3538952 | tf_op jit(solution)/shard_map/ppermute | solution.py:482
  83.8 11.7 %collective-permute-start.6 = (f32[1,2048]{1,0:T(1,128)S(1)}, f32[1,2048]{1,0:T(1,128)S(1)}, u32[]{:S(2)}, u32[]{:S(2)}) collective-permute-start(f32[1,2048]{1,0:T(1,128)S(1)} %get-tuple-element.62), channel_id=1, source_target_pairs={{8,16},{16,8},{24,32},{32,24},{40,48},{48,40},{56,64},{64,56},{72,... | collective-permute-start | bytes 24584 | tf_op jit(solution)/shard_map/ppermute | solution.py:424
  87.8 7.7 %collective-permute-start.7 = (f32[1,2048]{1,0:T(1,128)S(1)}, f32[1,2048]{1,0:T(1,128)S(1)}, u32[]{:S(2)}, u32[]{:S(2)}) collective-permute-start(f32[1,2048]{1,0:T(1,128)S(1)} %get-tuple-element.63), channel_id=1, source_target_pairs={{0,1},{1,0},{2,3},{3,2},{4,5},{5,4},{6,7},{7,6},{8,9},{9,8},{10,11... | collective-permute-start | bytes 24584 | tf_op jit(solution)/shard_map/ppermute | solution.py:425
  90.6 5.6 %collective-permute-start.8 = (f32[1,2048]{1,0:T(1,128)S(1)}, f32[1,2048]{1,0:T(1,128)S(1)}, u32[]{:S(2)}, u32[]{:S(2)}) collective-permute-start(f32[1,2048]{1,0:T(1,128)S(1)} %get-tuple-element.64), channel_id=1, source_target_pairs={{1,2},{2,1},{3,4},{4,3},{5,6},{6,5},{7,0},{0,7},{9,10},{10,9},{11,... | collective-permute-start | bytes 24584 | tf_op jit(solution)/shard_map/ppermute | solution.py:426
  92.9 3.5 %collective-permute-start.9 = (f32[1,2048]{1,0:T(1,128)S(1)}, f32[1,2048]{1,0:T(1,128)S(1)}, u32[]{:S(2)}, u32[]{:S(2)}) collective-permute-start(f32[1,2048]{1,0:T(1,128)S(1)} %get-tuple-element.65), channel_id=1, source_target_pairs={{0,8},{8,0},{16,24},{24,16},{32,40},{40,32},{48,56},{56,48},{64,72... | collective-permute-start | bytes 24584 | tf_op jit(solution)/shard_map/ppermute | solution.py:427
  132.6 11.5 %collective-permute-start.10 = (f32[1,2048]{1,0:T(1,128)S(1)}, f32[1,2048]{1,0:T(1,128)S(1)}, u32[]{:S(2)}, u32[]{:S(2)}) collective-permute-start(f32[1,2048]{1,0:T(1,128)S(1)} %get-tuple-element.71), channel_id=1, source_target_pairs={{8,16},{16,8},{24,32},{32,24},{40,48},{48,40},{56,64},{64,56},{72,... | collective-permute-start | bytes 24584 | tf_op jit(solution)/shard_map/ppermute | solution.py:424
  136.7 7.4 %collective-permute-start.11 = (f32[1,2048]{1,0:T(1,128)S(1)}, f32[1,2048]{1,0:T(1,128)S(1)}, u32[]{:S(2)}, u32[]{:S(2)}) collective-permute-start(f32[1,2048]{1,0:T(1,128)S(1)} %get-tuple-element.72), channel_id=1, source_target_pairs={{0,1},{1,0},{2,3},{3,2},{4,5},{5,4},{6,7},{7,6},{8,9},{9,8},{10,11... | collective-permute-start | bytes 24584 | tf_op jit(solution)/shard_map/ppermute | solution.py:425
  139.5 5.6 %collective-permute-start.12 = (f32[1,2048]{1,0:T(1,128)S(1)}, f32[1,2048]{1,0:T(1,128)S(1)}, u32[]{:S(2)}, u32[]{:S(2)}) collective-permute-start(f32[1,2048]{1,0:T(1,128)S(1)} %get-tuple-element.73), channel_id=1, source_target_pairs={{1,2},{2,1},{3,4},{4,3},{5,6},{6,5},{7,0},{0,7},{9,10},{10,9},{11,... | collective-permute-start | bytes 24584 | tf_op jit(solution)/shard_map/ppermute | solution.py:426
  141.8 3.4 %collective-permute-start.13 = (f32[1,2048]{1,0:T(1,128)S(1)}, f32[1,2048]{1,0:T(1,128)S(1)}, u32[]{:S(2)}, u32[]{:S(2)}) collective-permute-start(f32[1,2048]{1,0:T(1,128)S(1)} %get-tuple-element.74), channel_id=1, source_target_pairs={{0,8},{8,0},{16,24},{24,16},{32,40},{40,32},{48,56},{56,48},{64,72... | collective-permute-start | bytes 24584 | tf_op jit(solution)/shard_map/ppermute | solution.py:427

commit v4 on v3

--- a/solution.py
+++ b/solution.py
@@ -167,8 +167,8 @@
     )):
         copies.append(pltpu.make_async_copy(source, target, sems.at[i]))
         copies[-1].start()
-    copies[0].wait()
-    copies[1].wait()
+    for copy in copies:
+        copy.wait()
     spread_x = (iota((16, PLANE), 0) == (iota((16, PLANE), 1) >> 4)).astype(F32)
     spread_y = (iota((16, PLANE), 0) == (iota((16, PLANE), 1) & 15)).astype(F32)
     wide_x = dot_full(mode_x_ref[...], spread_x)
@@ -179,23 +179,18 @@
         here = slice(16 * i, 16 * i + 16)
         for k, part in enumerate(thirds(wide_x[i : i + 1] * wide_y) + thirds(tall_x[i : i + 1] * tall_y)):
             planes_ref[k, here] = part
-    copies[2].wait()
     mode_z = mode_z_ref[...]
     for k, part in enumerate(thirds(mode_z) + thirds(mode_z.T)):
         depths_ref[k] = part
     planes = [planes_ref[i] for i in range(6)]
     depths = [depths_ref[i] for i in range(6)]
 
-    copies[3].wait()
     line = dot_full(eigen_ref[:, 0:16], spread_x) + dot_full(eigen_ref[:, 16:32], spread_y)
     diagonal = iota((DEPTH, DEPTH), 0) == iota((DEPTH, DEPTH), 1)
     column = jnp.sum(jnp.where(diagonal, eigen_ref[:, 32:160], 0.0), axis=1, keepdims=True)
     lam_inv = 1.0 / (line + column)
     fields_ref[0] = lam_inv
 
-    copies[4].wait()
-    copies[8].wait()
-    copies[9].wait()
     spread_c = (iota((16, PLANE), 0) == ((iota((16, PLANE), 1) >> 6) * 4 + ((iota((16, PLANE), 1) >> 2) & 3))).astype(BF16)
     spread_d = (iota((DEPTH, 32), 1) == (iota((DEPTH, 32), 0) >> 2)).astype(BF16)
     small = classes_ref[...].astype(F32).astype(BF16)
@@ -217,9 +212,6 @@
     corners_ref[8:16, 0:DEPTH] = (dot(hot_d, depths[0]) + (dot(hot_d, depths[1]) + dot(hot_d, depths[2]))) * corner_root
     corners_ref[8:16, DEPTH:] = jnp.zeros((8, PLANE - DEPTH), F32)
 
-    copies[5].wait()
-    copies[6].wait()
-    copies[7].wait()
     weights = forward(loads_ref[...].T * root, planes, depths) * lam_inv
     high, low = split(backward(weights, planes, depths) * root)
     gather([(high, low), (class_part,)], rows_ref, [near_ref.at[0], cls_ref])

time: 148 us -> 147 us (level)
  no operation moved by 1% of the time
where the time goes in v4:
time: 147 us; the launch traced here: 146 us
  starting transfers between devices  62.3 us (42%)
  blocking collectives  57.6 us (39%)
  Pallas kernels  20.7 us (14%)
  waiting for transfers between devices  2.62 us (2%)
  local copies, waits for them, and re-layouts  2.08 us (1%)
    all_to_all x2, blocking collectives, total(): return (lax.all_to_all(send, ('x', 'y'), 0, 0, tiled=True), held)  30.4 us
    all_to_all x2, blocking collectives, total(): got = lax.all_to_all(send, ('z', 'core'), 0, 0, tiled=True)  27.1 us
    pallas_call x8, Pallas kernels, call(): pl.pallas_call(kernel, name=name, out_shape=[jax.ShapeDtypeStruct(*o) for...  20.7 us
    ppermute x3, starting transfers between devices, exchange(): mate = lax.ppermute(messages[3], sub, pairing(NSUB, 0))  19.2 us
    ppermute x3, starting transfers between devices, exchange(): far_sub = lax.ppermute(messages[0], sub, pairing(NSUB, 1))  12.9 us
    ppermute x3, starting transfers between devices, exchange(): near_col = lax.ppermute(messages[1], 'y', pairing(NY, 0))  9.17 us
    ppermute x3, starting transfers between devices, exchange(): far_col = lax.ppermute(messages[2], 'y', pairing(NY, 1))  8.82 us
    all_to_all x1, starting transfers between devices, on_device(): own = lax.all_to_all(quarter, 'y', 0, 0, tiled=True)  7.65 us
  transfers between devices with their start and end apart: 15, of which 4 were waited for; matrix products, arithmetic and copies ran while one was open for 0% of the time, Pallas kernels for 6%

profile of v4, /device:TPU:1, one launch (start us, length us, event | category | flops | bytes accessed | tf_op | source)
XLA Modules:
  0.0 146.3 jit_solution(4052753719440859556)
XLA Ops:
  0.7 0.9 copy-done
  1.6 0.9 broadcast_in_dim.12
  2.5 7.7 %all-to-all-start = ((f32[8,24,768]{2,1,0:T(8,128)}), f32[8,24,768]{2,1,0:T(8,128)S(1)}, u32[]{:S(2)}, u32[]{:S(2)}) async-start(f32[8,24,768]{2,1,0:T(8,128)} %broadcast_in_dim.12), calls=%async_computation | async-start | bytes 1179648 | tf_op jit(solution)/shard_map/all_to_all | solution.py:429
  10.1 5.0 %start.1 = (bf16[6,256,256]{2,1,0:T(8,128)(2,1)S(1)}, bf16[6,128,128]{2,1,0:T(8,128)(2,1)S(1)}, f32[2,128,256]{2,1,0:T(8,128)S(1)}, f32[16,256]{1,0:T(8,128)S(1)...) custom-call(f32[16,16]{1,0:T(8,128)} %bitcast.58, ...), custom_call_target="tpu_custom_call" | custom-call | flops 2000000000 | bytes 4000000 | tf_op jit(solution)/shard_map/start/pallas_call | solution.py:394
  15.1 4.8 %collective-permute-start = (f32[2,2048]{1,0:T(2,128)S(1)}, f32[2,2048]{1,0:T(2,128)S(1)}, u32[]{:S(2)}, u32[]{:S(2)}) collective-permute-start(f32[2,2048]{1,0:T(2,128)S(1)} %get-tuple-element.42), channel_id=1, source_target_pairs={{8,16},{16,8},{24,32},{32,24},{40,48},{48,40},{56,64},{64,56},{72,... | collective-permute-start | bytes 49160 | tf_op jit(solution)/shard_map/ppermute | solution.py:416
  20.0 3.6 %collective-permute-start.1 = (f32[2,2048]{1,0:T(2,128)S(1)}, f32[2,2048]{1,0:T(2,128)S(1)}, u32[]{:S(2)}, u32[]{:S(2)}) collective-permute-start(f32[2,2048]{1,0:T(2,128)S(1)} %get-tuple-element.43), channel_id=1, source_target_pairs={{0,1},{1,0},{2,3},{3,2},{4,5},{5,4},{6,7},{7,6},{8,9},{9,8},{10,11... | collective-permute-start | bytes 49160 | tf_op jit(solution)/shard_map/ppermute | solution.py:417
  23.6 4.3 %collective-permute-start.2 = (f32[2,2048]{1,0:T(2,128)S(1)}, f32[2,2048]{1,0:T(2,128)S(1)}, u32[]{:S(2)}, u32[]{:S(2)}) collective-permute-start(f32[2,2048]{1,0:T(2,128)S(1)} %get-tuple-element.44), channel_id=1, source_target_pairs={{1,2},{2,1},{3,4},{4,3},{5,6},{6,5},{7,0},{0,7},{9,10},{10,9},{11,... | collective-permute-start | bytes 49160 | tf_op jit(solution)/shard_map/ppermute | solution.py:418
  27.9 14.2 %collective-permute-start.3 = (f32[2,2048]{1,0:T(2,128)S(1)}, f32[2,2048]{1,0:T(2,128)S(1)}, u32[]{:S(2)}, u32[]{:S(2)}) collective-permute-start(f32[2,2048]{1,0:T(2,128)S(1)} %get-tuple-element.45), channel_id=1, source_target_pairs={{0,8},{8,0},{16,24},{24,16},{32,40},{40,32},{48,56},{56,48},{64,72... | collective-permute-start | bytes 49160 | tf_op jit(solution)/shard_map/ppermute | solution.py:419
  42.2 0.8 collective-permute-done.3.m3_ref
  43.0 1.9 %collective-permute-start.4 = (f32[192,768]{1,0:T(8,128)S(1)}, f32[192,768]{1,0:T(8,128)S(1)}, u32[]{:S(2)}, u32[]{:S(2)}) collective-permute-start(f32[192,768]{1,0:T(8,128)S(1)} %bitcast.31), channel_id=1, source_target_pairs={{0,192},{192,0},{384,576},{576,384},{1,193},{193,1},{385,577},{577... | collective-permute-start | bytes 1769480 | tf_op jit(solution)/shard_map/ppermute | solution.py:457
  44.9 3.2 %first.1 = (f32[2,4,2048]{2,1,0:T(4,128)S(1)}, f32[128,256]{1,0:T(8,128)S(1)}, f32[24,128]{1,0:T(8,128)S(1)}) custom-call(s32[2,4]{1,0:T(2,128)S(1)} %bitcast.44, s32[8]{0:T(128)S(1)} %bitcast.49, s32[4,2048]{1,0:T(4,128)S(1)} %get-tuple-element.40.rows_ref, f32[2,4,2048]{2,1,0:T(4,128)S(1)} %get-tuple-element.41.near_ref, ...), custom_call_target="tpu_custom_call" | custom-call | flops 2000000000 | bytes 4000000 | tf_op jit(solution)/shard_map/first/pallas_call | solution.py:394
  48.1 13.2 %all_to_all.55 = f32[24,1,128]{2,1,0:T(1,128)S(1)} all-to-all(f32[24,1,128]{2,1,0:T(1,128)S(1)} %bitcast.42), channel_id=1, replica_groups=mesh['x'=4,'z'=12,'core'=2,'y'=8] {'z','core'}, dimensions={0} | all-to-all | bytes 24576 | tf_op jit(solution)/shard_map/all_to_all | solution.py:460
  61.3 2.6 %collective-permute-start.5 = (f32[384,768]{1,0:T(8,128)S(1)}, f32[384,768]{1,0:T(8,128)S(1)}, u32[]{:S(2)}, u32[]{:S(2)}) collective-permute-start(f32[384,768]{1,0:T(8,128)S(1)} %pad_maximum_fusion), channel_id=1, source_target_pairs={{0,8},{8,0},{16,24},{24,16},{32,40},{40,32},{48,56},{56,48},{64,72... | collective-permute-start | bytes 3538952 | tf_op jit(solution)/shard_map/ppermute | solution.py:474
  63.9 0.2 relay.2
  64.2 15.4 %all_to_all.56 = f32[32,1,896]{2,1,0:T(1,128)S(1)} all-to-all(f32[32,1,896]{2,1,0:T(1,128)S(1)} %copy.15), channel_id=1, replica_groups=mesh['x'=4,'z'=12,'core'=2,'y'=8] {'x','y'}, dimensions={0} | all-to-all | bytes 229376 | tf_op jit(solution)/shard_map/all_to_all | solution.py:463
  79.7 3.6 %coarse.2 = (f32[4,2048]{1,0:T(4,128)S(1)}, f32[8,128]{1,0:T(8,128)S(1)}, f32[1,2048]{1,0:T(1,128)S(1)}, f32[1,2048]{1,0:T(1,128)S(1)}, f32[1,2048]{1,0:T(1,128)S(1)}, /*index=5*/f32[1,2048]{1,0:T(1,128)S(1)}) custom-call(s32[2,4]{1,0:T(2,128)S(1)} %bitcast.45, s32[8]{0:T(128)S(1)} %bitcast.50, s32[4,2048]{1,0:T(4,128)S(1)} %get-tuple-element.40.rows_ref, ...), custom_call_target="tpu_custom_call" | custom-call | flops 2000000000 | bytes 4000000 | tf_op jit(solution)/shard_map/coarse/pallas_call | solution.py:394
  83.3 4.0 %collective-permute-start.6 = (f32[1,2048]{1,0:T(1,128)S(1)}, f32[1,2048]{1,0:T(1,128)S(1)}, u32[]{:S(2)}, u32[]{:S(2)}) collective-permute-start(f32[1,2048]{1,0:T(1,128)S(1)} %get-tuple-element.62), channel_id=1, source_target_pairs={{8,16},{16,8},{24,32},{32,24},{40,48},{48,40},{56,64},{64,56},{72,... | collective-permute-start | bytes 24584 | tf_op jit(solution)/shard_map/ppermute | solution.py:416
  87.3 2.7 %collective-permute-start.7 = (f32[1,2048]{1,0:T(1,128)S(1)}, f32[1,2048]{1,0:T(1,128)S(1)}, u32[]{:S(2)}, u32[]{:S(2)}) collective-permute-start(f32[1,2048]{1,0:T(1,128)S(1)} %get-tuple-element.63), channel_id=1, source_target_pairs={{0,1},{1,0},{2,3},{3,2},{4,5},{5,4},{6,7},{7,6},{8,9},{9,8},{10,11... | collective-permute-start | bytes 24584 | tf_op jit(solution)/shard_map/ppermute | solution.py:417
  90.0 2.3 %collective-permute-start.8 = (f32[1,2048]{1,0:T(1,128)S(1)}, f32[1,2048]{1,0:T(1,128)S(1)}, u32[]{:S(2)}, u32[]{:S(2)}) collective-permute-start(f32[1,2048]{1,0:T(1,128)S(1)} %get-tuple-element.64), channel_id=1, source_target_pairs={{1,2},{2,1},{3,4},{4,3},{5,6},{6,5},{7,0},{0,7},{9,10},{10,9},{11,... | collective-permute-start | bytes 24584 | tf_op jit(solution)/shard_map/ppermute | solution.py:418
  92.3 2.7 %collective-permute-start.9 = (f32[1,2048]{1,0:T(1,128)S(1)}, f32[1,2048]{1,0:T(1,128)S(1)}, u32[]{:S(2)}, u32[]{:S(2)}) collective-permute-start(f32[1,2048]{1,0:T(1,128)S(1)} %get-tuple-element.65), channel_id=1, source_target_pairs={{0,8},{8,0},{16,24},{24,16},{32,40},{40,32},{48,56},{56,48},{64,72... | collective-permute-start | bytes 24584 | tf_op jit(solution)/shard_map/ppermute | solution.py:419
  95.0 0.6 collective-permute-done.8.m2_ref
  95.8 3.3 %second.1 = (f32[4,4,2048]{2,1,0:T(4,128)S(1)}, f32[128,256]{1,0:T(8,128)S(1)}, f32[24,128]{1,0:T(8,128)S(1)}) custom-call(s32[2,4]{1,0:T(2,128)S(1)} %bitcast.46, s32[8]{0:T(128)S(1)} %bitcast.51, s32[4,2048]{1,0:T(4,128)S(1)} %get-tuple-element.40.rows_ref, f32[4,2048]{1,0:T(4,128)S(1)} %get-tuple-element.60.near_ref, ...), custom_call_target="tpu_custom_call" | custom-call | flops 2000000000 | bytes 4000000 | tf_op jit(solution)/shard_map/second/pallas_call | solution.py:394
  99.1 14.0 %all_to_all.57 = f32[24,1,128]{2,1,0:T(1,128)S(1)} all-to-all(f32[24,1,128]{2,1,0:T(1,128)S(1)} %bitcast.41), channel_id=1, replica_groups=mesh['x'=4,'z'=12,'core'=2,'y'=8] {'z','core'}, dimensions={0} | all-to-all | bytes 24576 | tf_op jit(solution)/shard_map/all_to_all | solution.py:460
  113.1 0.2 relay.3
  113.4 15.0 %all_to_all.58 = f32[32,1,896]{2,1,0:T(1,128)S(1)} all-to-all(f32[32,1,896]{2,1,0:T(1,128)S(1)} %copy.17), channel_id=1, replica_groups=mesh['x'=4,'z'=12,'core'=2,'y'=8] {'x','y'}, dimensions={0} | all-to-all | bytes 229376 | tf_op jit(solution)/shard_map/all_to_all | solution.py:463
  128.4 3.6 %coarse.3 = (f32[4,2048]{1,0:T(4,128)S(1)}, f32[8,128]{1,0:T(8,128)S(1)}, f32[1,2048]{1,0:T(1,128)S(1)}, f32[1,2048]{1,0:T(1,128)S(1)}, f32[1,2048]{1,0:T(1,128)S(1)}, /*index=5*/f32[1,2048]{1,0:T(1,128)S(1)}) custom-call(s32[2,4]{1,0:T(2,128)S(1)} %bitcast.47, s32[8]{0:T(128)S(1)} %bitcast.52, s32[4,2048]{1,0:T(4,128)S(1)} %get-tuple-element.40.rows_ref, ...), custom_call_target="tpu_custom_call" | custom-call | flops 2000000000 | bytes 4000000 | tf_op jit(solution)/shard_map/coarse/pallas_call | solution.py:394
  132.0 4.1 %collective-permute-start.10 = (f32[1,2048]{1,0:T(1,128)S(1)}, f32[1,2048]{1,0:T(1,128)S(1)}, u32[]{:S(2)}, u32[]{:S(2)}) collective-permute-start(f32[1,2048]{1,0:T(1,128)S(1)} %get-tuple-element.71), channel_id=1, source_target_pairs={{8,16},{16,8},{24,32},{32,24},{40,48},{48,40},{56,64},{64,56},{72,... | collective-permute-start | bytes 24584 | tf_op jit(solution)/shard_map/ppermute | solution.py:416
  136.1 2.8 %collective-permute-start.11 = (f32[1,2048]{1,0:T(1,128)S(1)}, f32[1,2048]{1,0:T(1,128)S(1)}, u32[]{:S(2)}, u32[]{:S(2)}) collective-permute-start(f32[1,2048]{1,0:T(1,128)S(1)} %get-tuple-element.72), channel_id=1, source_target_pairs={{0,1},{1,0},{2,3},{3,2},{4,5},{5,4},{6,7},{7,6},{8,9},{9,8},{10,11... | collective-permute-start | bytes 24584 | tf_op jit(solution)/shard_map/ppermute | solution.py:417
  138.9 2.2 %collective-permute-start.12 = (f32[1,2048]{1,0:T(1,128)S(1)}, f32[1,2048]{1,0:T(1,128)S(1)}, u32[]{:S(2)}, u32[]{:S(2)}) collective-permute-start(f32[1,2048]{1,0:T(1,128)S(1)} %get-tuple-element.73), channel_id=1, source_target_pairs={{1,2},{2,1},{3,4},{4,3},{5,6},{6,5},{7,0},{0,7},{9,10},{10,9},{11,... | collective-permute-start | bytes 24584 | tf_op jit(solution)/shard_map/ppermute | solution.py:418
  141.2 2.3 %collective-permute-start.13 = (f32[1,2048]{1,0:T(1,128)S(1)}, f32[1,2048]{1,0:T(1,128)S(1)}, u32[]{:S(2)}, u32[]{:S(2)}) collective-permute-start(f32[1,2048]{1,0:T(1,128)S(1)} %get-tuple-element.74), channel_id=1, source_target_pairs={{0,8},{8,0},{16,24},{24,16},{32,40},{40,32},{48,56},{56,48},{64,72... | collective-permute-start | bytes 24584 | tf_op jit(solution)/shard_map/ppermute | solution.py:419
  143.6 1.0 collective-permute-done.12.m2_ref
  144.6 1.7 %end.1 = (f32[4,2048]{1,0:T(4,128)}, f32[4,2048]{1,0:T(4,128)}) custom-call(s32[2,4]{1,0:T(2,128)S(1)} %bitcast.48, f32[4,2048]{1,0:T(4,128)S(1)} %get-tuple-element.69.near_ref, f32[8,128]{1,0:T(8,128)S(1)} %get-tuple-element.70.sums_ref, f32[8,128]{1,0:T(8,128)S(1)} %get-tuple-element.61.sums_ref.first_ref, f32[1,2048]{1,0:T(1,128)S(1)} %collective-permute-done.10.m0_ref, ...), custom_call_target="tpu_custom_call" | custom-call | flops 1000 | bytes 4000000 | tf_op jit(solution)/shard_map/end/pallas_call | solution.py:394
  (23 shorter events, 0.5 us)
Async XLA Ops:
  0.6 1.0 copy-start
  2.5 40.5 %all-to-all-start = ((f32[8,24,768]{2,1,0:T(8,128)}), f32[8,24,768]{2,1,0:T(8,128)S(1)}, u32[]{:S(2)}, u32[]{:S(2)}) async-start(f32[8,24,768]{2,1,0:T(8,128)} %broadcast_in_dim.12), calls=%async_computation | async-start | bytes 1179648 | tf_op jit(solution)/shard_map/all_to_all | solution.py:429
  10.1 34.8 %copy-start.1 = (s32[1,1,4,2]{2,3,1,0:T(2,128)S(1)}, s32[1,1,4,2]{2,3,1,0:T(2,128)}, u32[]{:S(2)}) copy-start(s32[1,1,4,2]{2,3,1,0:T(2,128)} %param.19) | copy-start | bytes 100
  10.1 34.8 %copy-start.2 = (s32[1,1,8]{2,1,0:T(1,128)S(1)}, s32[1,1,8]{2,1,0:T(1,128)}, u32[]{:S(2)}) copy-start(s32[1,1,8]{2,1,0:T(1,128)} %param.21) | copy-start | bytes 100
  15.1 27.1 %collective-permute-start = (f32[2,2048]{1,0:T(2,128)S(1)}, f32[2,2048]{1,0:T(2,128)S(1)}, u32[]{:S(2)}, u32[]{:S(2)}) collective-permute-start(f32[2,2048]{1,0:T(2,128)S(1)} %get-tuple-element.42), channel_id=1, source_target_pairs={{8,16},{16,8},{24,32},{32,24},{40,48},{48,40},{56,64},{64,56},{72,... | collective-permute-start | bytes 49160 | tf_op jit(solution)/shard_map/ppermute | solution.py:416
  20.0 22.2 %collective-permute-start.1 = (f32[2,2048]{1,0:T(2,128)S(1)}, f32[2,2048]{1,0:T(2,128)S(1)}, u32[]{:S(2)}, u32[]{:S(2)}) collective-permute-start(f32[2,2048]{1,0:T(2,128)S(1)} %get-tuple-element.43), channel_id=1, source_target_pairs={{0,1},{1,0},{2,3},{3,2},{4,5},{5,4},{6,7},{7,6},{8,9},{9,8},{10,11... | collective-permute-start | bytes 49160 | tf_op jit(solution)/shard_map/ppermute | solution.py:417
  23.6 18.6 %collective-permute-start.2 = (f32[2,2048]{1,0:T(2,128)S(1)}, f32[2,2048]{1,0:T(2,128)S(1)}, u32[]{:S(2)}, u32[]{:S(2)}) collective-permute-start(f32[2,2048]{1,0:T(2,128)S(1)} %get-tuple-element.44), channel_id=1, source_target_pairs={{1,2},{2,1},{3,4},{4,3},{5,6},{6,5},{7,0},{0,7},{9,10},{10,9},{11,... | collective-permute-start | bytes 49160 | tf_op jit(solution)/shard_map/ppermute | solution.py:418
  27.9 15.1 %collective-permute-start.3 = (f32[2,2048]{1,0:T(2,128)S(1)}, f32[2,2048]{1,0:T(2,128)S(1)}, u32[]{:S(2)}, u32[]{:S(2)}) collective-permute-start(f32[2,2048]{1,0:T(2,128)S(1)} %get-tuple-element.45), channel_id=1, source_target_pairs={{0,8},{8,0},{16,24},{24,16},{32,40},{40,32},{48,56},{56,48},{64,72... | collective-permute-start | bytes 49160 | tf_op jit(solution)/shard_map/ppermute | solution.py:419
  43.0 18.3 %collective-permute-start.4 = (f32[192,768]{1,0:T(8,128)S(1)}, f32[192,768]{1,0:T(8,128)S(1)}, u32[]{:S(2)}, u32[]{:S(2)}) collective-permute-start(f32[192,768]{1,0:T(8,128)S(1)} %bitcast.31), channel_id=1, source_target_pairs={{0,192},{192,0},{384,576},{576,384},{1,193},{193,1},{385,577},{577... | collective-permute-start | bytes 1769480 | tf_op jit(solution)/shard_map/ppermute | solution.py:457
  61.3 18.3 %collective-permute-start.5 = (f32[384,768]{1,0:T(8,128)S(1)}, f32[384,768]{1,0:T(8,128)S(1)}, u32[]{:S(2)}, u32[]{:S(2)}) collective-permute-start(f32[384,768]{1,0:T(8,128)S(1)} %pad_maximum_fusion), channel_id=1, source_target_pairs={{0,8},{8,0},{16,24},{24,16},{32,40},{40,32},{48,56},{56,48},{64,72... | collective-permute-start | bytes 3538952 | tf_op jit(solution)/shard_map/ppermute | solution.py:474
  83.3 11.7 %collective-permute-start.6 = (f32[1,2048]{1,0:T(1,128)S(1)}, f32[1,2048]{1,0:T(1,128)S(1)}, u32[]{:S(2)}, u32[]{:S(2)}) collective-permute-start(f32[1,2048]{1,0:T(1,128)S(1)} %get-tuple-element.62), channel_id=1, source_target_pairs={{8,16},{16,8},{24,32},{32,24},{40,48},{48,40},{56,64},{64,56},{72,... | collective-permute-start | bytes 24584 | tf_op jit(solution)/shard_map/ppermute | solution.py:416
  87.3 7.7 %collective-permute-start.7 = (f32[1,2048]{1,0:T(1,128)S(1)}, f32[1,2048]{1,0:T(1,128)S(1)}, u32[]{:S(2)}, u32[]{:S(2)}) collective-permute-start(f32[1,2048]{1,0:T(1,128)S(1)} %get-tuple-element.63), channel_id=1, source_target_pairs={{0,1},{1,0},{2,3},{3,2},{4,5},{5,4},{6,7},{7,6},{8,9},{9,8},{10,11... | collective-permute-start | bytes 24584 | tf_op jit(solution)/shard_map/ppermute | solution.py:417
  90.0 5.6 %collective-permute-start.8 = (f32[1,2048]{1,0:T(1,128)S(1)}, f32[1,2048]{1,0:T(1,128)S(1)}, u32[]{:S(2)}, u32[]{:S(2)}) collective-permute-start(f32[1,2048]{1,0:T(1,128)S(1)} %get-tuple-element.64), channel_id=1, source_target_pairs={{1,2},{2,1},{3,4},{4,3},{5,6},{6,5},{7,0},{0,7},{9,10},{10,9},{11,... | collective-permute-start | bytes 24584 | tf_op jit(solution)/shard_map/ppermute | solution.py:418
  92.3 3.5 %collective-permute-start.9 = (f32[1,2048]{1,0:T(1,128)S(1)}, f32[1,2048]{1,0:T(1,128)S(1)}, u32[]{:S(2)}, u32[]{:S(2)}) collective-permute-start(f32[1,2048]{1,0:T(1,128)S(1)} %get-tuple-element.65), channel_id=1, source_target_pairs={{0,8},{8,0},{16,24},{24,16},{32,40},{40,32},{48,56},{56,48},{64,72... | collective-permute-start | bytes 24584 | tf_op jit(solution)/shard_map/ppermute | solution.py:419
  132.0 11.5 %collective-permute-start.10 = (f32[1,2048]{1,0:T(1,128)S(1)}, f32[1,2048]{1,0:T(1,128)S(1)}, u32[]{:S(2)}, u32[]{:S(2)}) collective-permute-start(f32[1,2048]{1,0:T(1,128)S(1)} %get-tuple-element.71), channel_id=1, source_target_pairs={{8,16},{16,8},{24,32},{32,24},{40,48},{48,40},{56,64},{64,56},{72,... | collective-permute-start | bytes 24584 | tf_op jit(solution)/shard_map/ppermute | solution.py:416
  136.1 7.4 %collective-permute-start.11 = (f32[1,2048]{1,0:T(1,128)S(1)}, f32[1,2048]{1,0:T(1,128)S(1)}, u32[]{:S(2)}, u32[]{:S(2)}) collective-permute-start(f32[1,2048]{1,0:T(1,128)S(1)} %get-tuple-element.72), channel_id=1, source_target_pairs={{0,1},{1,0},{2,3},{3,2},{4,5},{5,4},{6,7},{7,6},{8,9},{9,8},{10,11... | collective-permute-start | bytes 24584 | tf_op jit(solution)/shard_map/ppermute | solution.py:417
  138.9 5.6 %collective-permute-start.12 = (f32[1,2048]{1,0:T(1,128)S(1)}, f32[1,2048]{1,0:T(1,128)S(1)}, u32[]{:S(2)}, u32[]{:S(2)}) collective-permute-start(f32[1,2048]{1,0:T(1,128)S(1)} %get-tuple-element.73), channel_id=1, source_target_pairs={{1,2},{2,1},{3,4},{4,3},{5,6},{6,5},{7,0},{0,7},{9,10},{10,9},{11,... | collective-permute-start | bytes 24584 | tf_op jit(solution)/shard_map/ppermute | solution.py:418
  141.2 3.4 %collective-permute-start.13 = (f32[1,2048]{1,0:T(1,128)S(1)}, f32[1,2048]{1,0:T(1,128)S(1)}, u32[]{:S(2)}, u32[]{:S(2)}) collective-permute-start(f32[1,2048]{1,0:T(1,128)S(1)} %get-tuple-element.74), channel_id=1, source_target_pairs={{0,8},{8,0},{16,24},{24,16},{32,40},{40,32},{48,56},{56,48},{64,72... | collective-permute-start | bytes 24584 | tf_op jit(solution)/shard_map/ppermute | solution.py:419
